TPU v7x, 768 devices: a whole 4x8x12 slice. The times are simulated.
768 devices in a mesh: gx: 192 (over x, z_hi, y, core), gz: 4 (over z_lo).
Axes of the slice: x: 4, y: 8, z: 12 (z_hi: 3, z_lo: 4; z = z_hi * 4 + z_lo), core: 2. Of those that a mesh axis runs over, the one named last changes fastest.
Arguments:
- positions: float32 [3, 384, 64, 128], P(None, 'gx', 'gz'), may hold values from 0 to 1
- velocities: float32 [3, 384, 64, 128], P(None, 'gx', 'gz'), may hold values from -6 to 6
- forces: float32 [3, 384, 64, 128], P(None, 'gx', 'gz'), may hold values from -18 to 18
- charge: float32 [384, 64, 128], P('gx', 'gz'), may hold values from -3 to 3
- atom_type: int32 [384, 64, 128], P('gx', 'gz'), may hold values from 0 to 15
- bin_count: int32 [384, 64], P('gx', 'gz'), may hold values from 64 to 128
- exclusions: int32 [384, 64, 2, 16], P('gx', 'gz'), may hold values from 0 to 63, as said below
- repulsion: float32 [16, 16], replicated, may hold values from 0.5 to 5
Outputs:
- positions_out: float32 [3, 384, 64, 128], P(None, 'gx', 'gz')
- velocities_out: float32 [3, 384, 64, 128], P(None, 'gx', 'gz')
- forces_out: float32 [3, 384, 64, 128], P(None, 'gx', 'gz')
Inputs may be any that keep to these rules, and one draw needn't show every extreme that they name: `exclusions`: each listed pair names two different slots below 64 of its bin.
All inputs are finite; a program needn't handle non-finite values.
Results may differ from a plain program's by a relative error of at most 0.0003.
Values sent between devices are 32-bit elements; how exact they have to be, the bound alone decides.
No kernel may reach another device: no remote copies, remote signals or barrier semaphores. Data moves between devices by JAX's collectives and lax.ppermute only.
A program may use at most 32 MiB of HBM per device.

v0:
```python
import jax
import jax.numpy as jnp
from jax import lax
from jax.sharding import PartitionSpec as P

STEPS = 2


time_step = 0.05
core_sq = 0.09
block_depth = 4
half_shell = ((0, 1), (1, -1), (1, 0), (1, 1))


def extended_2(block, sides, width):
    for axis, dim in sides:
        count = lax.axis_size(axis)
        forward = [(i, i + 1) for i in range(count - 1)]
        backward = [(target, source) for source, target in forward]
        low = lax.ppermute(
            lax.slice_in_dim(block, block.shape[dim] - width, None, axis=dim), axis, forward
        )
        high = lax.ppermute(lax.slice_in_dim(block, 0, width, axis=dim), axis, backward)
        block = jnp.concatenate([low, block, high], axis=dim)
    return block


def from_behind(value, axis, steps):
    count = lax.axis_size(axis)
    first, last = (max(0, -steps), min(count, count - steps))
    return lax.ppermute(value, axis, [(source, source + steps) for source in range(first, last)])


def shifted(block, axis, distance):
    devices = range(lax.axis_size(axis))
    route = [((i - distance) % len(devices), i) for i in devices]
    return lax.ppermute(block, axis, route)


def pack_atoms(positions, charge, atom_type, bin_count):
    slot_ids = jnp.arange(positions.shape[-1], dtype=jnp.int32)
    is_live = slot_ids < bin_count[..., None]
    type_code = jnp.where(is_live, atom_type + 1, 0).astype(jnp.float32)
    live_charge = jnp.where(is_live, charge, 0.0)
    return jnp.concatenate([positions, live_charge[None], type_code[None]], axis=0)


def soft_table(own_code, partner_code, table_ext):
    levels = jnp.arange(table_ext.shape[0], dtype=jnp.float32)
    hot_own = (own_code[..., None] == levels).astype(jnp.float32)
    hot_other = (partner_code[..., None] == levels).astype(jnp.float32)
    by_rows = jnp.einsum("bik,kl->bil", hot_own, table_ext, precision=lax.Precision.HIGHEST)
    return jnp.einsum("bil,bjl->bij", by_rows, hot_other, precision=lax.Precision.HIGHEST)


def exclusion_keep(pair_list, slot_total):
    levels = jnp.arange(slot_total, dtype=jnp.int32)
    first_hot = (pair_list[:, 0, :, None] == levels).astype(jnp.float32)
    second_hot = (pair_list[:, 1, :, None] == levels).astype(jnp.float32)
    matches = jnp.einsum("bei,bej->bij", first_hot, second_hot, precision=lax.Precision.HIGHEST)
    matches = matches + jnp.swapaxes(matches, 1, 2)
    return (matches == 0.0).astype(jnp.float32)


def pair_terms(own_atoms, partner, shift_x, shift_z, table_ext, keep_mask):
    delta_x = own_atoms[0][:, :, None] - partner[0][:, None, :] - shift_x
    delta_y = own_atoms[1][:, :, None] - partner[1][:, None, :]
    delta_z = own_atoms[2][:, :, None] - partner[2][:, None, :] - shift_z
    dist_sq = delta_x * delta_x + delta_y * delta_y + delta_z * delta_z
    inside = jnp.maximum(1.0 - dist_sq, 0.0)
    inverse = lax.rsqrt(dist_sq + core_sq)
    coulomb = (
        own_atoms[3][:, :, None]
        * partner[3][:, None, :]
        * inside
        * inside
        * inverse
        * inverse
        * inverse
    )
    scalar = soft_table(own_atoms[4], partner[4], table_ext) * inside + coulomb
    if keep_mask is not None:
        scalar = scalar * keep_mask
    on_own = jnp.stack(
        [
            jnp.sum(scalar * delta_x, axis=2),
            jnp.sum(scalar * delta_y, axis=2),
            jnp.sum(scalar * delta_z, axis=2),
        ]
    )
    on_partner = -jnp.stack(
        [
            jnp.sum(scalar * delta_x, axis=1),
            jnp.sum(scalar * delta_y, axis=1),
            jnp.sum(scalar * delta_z, axis=1),
        ]
    )
    return (on_own, on_partner)


def tower_import(extended):
    return extended_2(extended, (("gz", 2),), 1)


def tower_return(rim_forces, offset):
    return from_behind(rim_forces, "gz", offset)


def block_forces(extended, exclusions, own_start, offsets, table_ext):
    columns = exclusions.shape[0]
    bin_depth = exclusions.shape[1]
    slot_total = extended.shape[-1]
    width = columns * block_depth

    def one_block(block_index):
        first_row = block_index * block_depth
        window = lax.dynamic_slice_in_dim(extended, first_row, block_depth + 2, 2)
        own_atoms = window[:, own_start : own_start + columns, 1 : block_depth + 1].reshape(
            5, width, slot_total
        )
        pair_list = lax.dynamic_slice_in_dim(exclusions, first_row, block_depth, 1)
        pair_list = pair_list.reshape(width, 2, pair_list.shape[-1])
        keep_mask = exclusion_keep(pair_list, slot_total)
        summed, unused = pair_terms(own_atoms, own_atoms, 0.0, 0.0, table_ext, keep_mask)
        reactions = []
        for shift_x, shift_z in offsets:
            partner = window[
                :,
                own_start + shift_x : own_start + shift_x + columns,
                1 + shift_z : 1 + shift_z + block_depth,
            ]
            on_own, on_partner = pair_terms(
                own_atoms,
                partner.reshape(5, width, slot_total),
                float(shift_x),
                float(shift_z),
                table_ext,
                None,
            )
            summed = summed + on_own
            reactions.append(on_partner.reshape(3, columns, block_depth, slot_total))
        summed = summed.reshape(3, columns, block_depth, slot_total)
        return (summed, jnp.stack(reactions))

    blocks = bin_depth // block_depth
    results = lax.map(one_block, jnp.arange(blocks, dtype=jnp.int32))
    summed_all, reaction_all = results
    summed_all = jnp.transpose(summed_all, (1, 2, 0, 3, 4)).reshape(
        3, columns, bin_depth, slot_total
    )
    reaction_all = jnp.transpose(reaction_all, (1, 2, 3, 0, 4, 5)).reshape(
        len(offsets), 3, columns, bin_depth, slot_total
    )
    return (summed_all, reaction_all)


def local(positions, velocities, forces, charge, atom_type, bin_count, exclusions, repulsion):
    table_ext = jnp.pad(0.5 * (repulsion + repulsion.T), ((1, 0), (1, 0)))
    columns = positions.shape[1]
    bin_depth = positions.shape[2]
    slot_total = positions.shape[3]
    for step_number in range(STEPS):
        velocities = velocities + 0.5 * time_step * forces
        positions = positions + time_step * velocities
        packed = pack_atoms(positions, charge, atom_type, bin_count)
        column = shifted(packed[:, :1], "gx", -1)
        extended = tower_import(jnp.concatenate([packed, column], axis=1))
        summed, reactions = block_forces(extended, exclusions, 0, half_shell, table_ext)
        on_ext = jnp.zeros((3, columns + 1, bin_depth + 2, slot_total), jnp.float32)
        on_ext = on_ext.at[:, :columns, 1 : bin_depth + 1].add(summed)
        on_ext = on_ext.at[:, :columns, 2:].add(reactions[0])
        on_ext = on_ext.at[:, 1:, :bin_depth].add(reactions[1])
        on_ext = on_ext.at[:, 1:, 1 : bin_depth + 1].add(reactions[2])
        on_ext = on_ext.at[:, 1:, 2:].add(reactions[3])
        from_above = tower_return(on_ext[:, :, :1], -1)
        from_below = tower_return(on_ext[:, :, bin_depth + 1 :], 1)
        on_ext = on_ext.at[:, :, bin_depth : bin_depth + 1].add(from_above)
        on_ext = on_ext.at[:, :, 1:2].add(from_below)
        returned = shifted(on_ext[:, columns:, 1 : bin_depth + 1], "gx", 1)
        forces = on_ext[:, :columns, 1 : bin_depth + 1].at[:, :1].add(returned)
        velocities = velocities + 0.5 * time_step * forces
    return (positions, velocities, forces)


def solution(mesh):
    return jax.shard_map(
        local,
        mesh=mesh,
        in_specs=(
            P(None, "gx", "gz", None),
            P(None, "gx", "gz", None),
            P(None, "gx", "gz", None),
            P("gx", "gz", None),
            P("gx", "gz", None),
            P("gx", "gz"),
            P("gx", "gz", None, None),
            P(),
        ),
        out_specs=(P(None, "gx", "gz", None), P(None, "gx", "gz", None), P(None, "gx", "gz", None)),
        check_vma=False,
    )
```

profile of v0, /device:TPU:64, one launch (start us, length us, event | category | flops | bytes accessed | tf_op | source)
XLA Modules:
  0.0 196.7 jit_solution(2349937618388148028)
XLA Ops:
  2.4 18.2 %collective-permute-start = (f32[5,1,16,128]{3,2,1,0:T(8,128)S(1)}, f32[5,1,16,128]{3,2,1,0:T(8,128)S(1)}, u32[]{:S(2)}, u32[]{:S(2)}) collective-permute-start(f32[5,1,16,128]{3,2,1,0:T(8,128)S(1)} %pad_maximum_fusion.9), channel_id=1, source_target_pairs={{4,0},{8,4},{12,8},{16,12},{20,16},{24,20},{28,24},{32,28},{36,32}... | collective-permute-start | bytes 122888 | tf_op jit(solution)/shard_map/ppermute | solution.py:37
  22.8 3.4 %collective-permute-start.1 = (f32[5,3,1,128]{3,2,1,0:T(1,128)S(1)}, f32[5,3,1,128]{3,2,1,0:T(1,128)S(1)}, u32[]{:S(2)}, u32[]{:S(2)}) collective-permute-start(f32[5,3,1,128]{3,2,1,0:T(1,128)S(1)} %get-tuple-element.667), channel_id=1, source_target_pairs={{0,1},{1,2},{2,3},{4,5},{5,6},{6,7},{8,9},{9,10},{10,11},{12,13},{... | collective-permute-start | bytes 23048 | tf_op jit(solution)/shard_map/ppermute | solution.py:20
  26.2 2.5 %collective-permute-start.2 = (f32[5,3,1,128]{3,2,1,0:T(1,128)S(1)}, f32[5,3,1,128]{3,2,1,0:T(1,128)S(1)}, u32[]{:S(2)}, u32[]{:S(2)}) collective-permute-start(f32[5,3,1,128]{3,2,1,0:T(1,128)S(1)} %get-tuple-element.668), channel_id=1, source_target_pairs={{1,0},{2,1},{3,2},{5,4},{6,5},{7,6},{9,8},{10,9},{11,10},{13,12},{... | collective-permute-start | bytes 23048 | tf_op jit(solution)/shard_map/ppermute | solution.py:23
  29.4 2.4 %collective-permute-done.2 = f32[5,3,1,128]{3,2,1,0:T(1,128)S(1)} collective-permute-done((f32[5,3,1,128]{3,2,1,0:T(1,128)S(1)}, f32[5,3,1,128]{3,2,1,0:T(1,128)S(1)}, u32[]{:S(2)}, u32[]{:S(2)}) %collective-permute-start.2) | collective-permute-done | bytes 7712 | tf_op jit(solution)/shard_map/ppermute | solution.py:23
  31.9 48.9 %while.46 = (s32[]{:T(128)}, f32[4,3,2,4,128]{4,3,2,1,0:T(4,128)S(1)}, f32[4,4,3,2,4,128]{5,4,3,2,1,0:T(4,128)S(1)}, s32[4]{0:T(128)S(1)}, s32[2,16,2,16]{3,1,0,...) while((s32[]{:T(128)}, ...), condition=%wide.region_28.29_spmd, body=%wide.region_0.28_spmd.sunk | while | flops 162505744 | bytes 6986204 | solution.py:146
  33.4 1.4 fusion.210
  34.9 1.5 fusion.209
  36.3 1.5 fusion.208
  38.5 3.4 %fusion.212 = (f32[8,128]{1,0:T(8,128)S(1)}, f32[8,128]{1,0:T(8,128)S(1)}, f32[8,128]{1,0:T(8,128)S(1)}, f32[8,128]{1,0:T(8,128)S(1)}, f32[8,128]{1,0:T(8,128)S(...) fusion(f32[8,128]{1,0:T(8,128)S(1)} %bitcast.468, ...), kind=kOutput, calls=%fused_computation.41.clone.1 | convolution fusion | flops 35647488 | bytes 2834432 | tf_op jit(solution)/shard_map/while/body/eval_jaxpr/bil,bjl->bij/dot_general | solution.py:53
  41.9 2.1 %fusion.213 = (f32[8,128]{1,0:T(8,128)S(1)}, f32[8,128]{1,0:T(8,128)S(1)}, f32[8,128]{1,0:T(8,128)S(1)}, f32[8,128]{1,0:T(8,128)S(1)}, f32[8,128]{1,0:T(8,128)S(1)}, /*index=5*/f32[8,128]{1,0:T(8,128)S(1)}) fusion(f32[8,128]{1,0:T(8,128)S(1)} %bitcast.449, f32[8,128]{1,0:T(8,128)S(1)} %bitcast.469, f32[8,128]{1,0:T(8,128)S(1)} %bitcast.447, ...), kind=kOutput, calls=%fused_computation.90.clone.1 | convolution fusion | flops 30682112 | bytes 131072 | tf_op jit(solution)/shard_map/while/body/eval_jaxpr/bil,bjl->bij/dot_general | solution.py:53
  47.1 1.5 fusion.209
  48.6 1.5 fusion.208
  50.7 3.4 %fusion.212 = (f32[8,128]{1,0:T(8,128)S(1)}, f32[8,128]{1,0:T(8,128)S(1)}, f32[8,128]{1,0:T(8,128)S(1)}, f32[8,128]{1,0:T(8,128)S(1)}, f32[8,128]{1,0:T(8,128)S(...) fusion(f32[8,128]{1,0:T(8,128)S(1)} %bitcast.468, ...), kind=kOutput, calls=%fused_computation.41.clone.1 | convolution fusion | flops 35647488 | bytes 2834432 | tf_op jit(solution)/shard_map/while/body/eval_jaxpr/bil,bjl->bij/dot_general | solution.py:53
  54.1 2.1 %fusion.213 = (f32[8,128]{1,0:T(8,128)S(1)}, f32[8,128]{1,0:T(8,128)S(1)}, f32[8,128]{1,0:T(8,128)S(1)}, f32[8,128]{1,0:T(8,128)S(1)}, f32[8,128]{1,0:T(8,128)S(1)}, /*index=5*/f32[8,128]{1,0:T(8,128)S(1)}) fusion(f32[8,128]{1,0:T(8,128)S(1)} %bitcast.449, f32[8,128]{1,0:T(8,128)S(1)} %bitcast.469, f32[8,128]{1,0:T(8,128)S(1)} %bitcast.447, ...), kind=kOutput, calls=%fused_computation.90.clone.1 | convolution fusion | flops 30682112 | bytes 131072 | tf_op jit(solution)/shard_map/while/body/eval_jaxpr/bil,bjl->bij/dot_general | solution.py:53
  57.9 1.4 fusion.210
  59.3 1.5 fusion.209
  60.8 1.5 fusion.208
  62.9 3.4 %fusion.212 = (f32[8,128]{1,0:T(8,128)S(1)}, f32[8,128]{1,0:T(8,128)S(1)}, f32[8,128]{1,0:T(8,128)S(1)}, f32[8,128]{1,0:T(8,128)S(1)}, f32[8,128]{1,0:T(8,128)S(...) fusion(f32[8,128]{1,0:T(8,128)S(1)} %bitcast.468, ...), kind=kOutput, calls=%fused_computation.41.clone.1 | convolution fusion | flops 35647488 | bytes 2834432 | tf_op jit(solution)/shard_map/while/body/eval_jaxpr/bil,bjl->bij/dot_general | solution.py:53
  66.3 2.1 %fusion.213 = (f32[8,128]{1,0:T(8,128)S(1)}, f32[8,128]{1,0:T(8,128)S(1)}, f32[8,128]{1,0:T(8,128)S(1)}, f32[8,128]{1,0:T(8,128)S(1)}, f32[8,128]{1,0:T(8,128)S(1)}, /*index=5*/f32[8,128]{1,0:T(8,128)S(1)}) fusion(f32[8,128]{1,0:T(8,128)S(1)} %bitcast.449, f32[8,128]{1,0:T(8,128)S(1)} %bitcast.469, f32[8,128]{1,0:T(8,128)S(1)} %bitcast.447, ...), kind=kOutput, calls=%fused_computation.90.clone.1 | convolution fusion | flops 30682112 | bytes 131072 | tf_op jit(solution)/shard_map/while/body/eval_jaxpr/bil,bjl->bij/dot_general | solution.py:53
  70.1 1.4 fusion.210
  71.5 1.5 fusion.209
  73.0 1.5 fusion.208
  75.1 3.4 %fusion.212 = (f32[8,128]{1,0:T(8,128)S(1)}, f32[8,128]{1,0:T(8,128)S(1)}, f32[8,128]{1,0:T(8,128)S(1)}, f32[8,128]{1,0:T(8,128)S(1)}, f32[8,128]{1,0:T(8,128)S(...) fusion(f32[8,128]{1,0:T(8,128)S(1)} %bitcast.468, ...), kind=kOutput, calls=%fused_computation.41.clone.1 | convolution fusion | flops 35647488 | bytes 2834432 | tf_op jit(solution)/shard_map/while/body/eval_jaxpr/bil,bjl->bij/dot_general | solution.py:53
  78.6 2.1 %fusion.213 = (f32[8,128]{1,0:T(8,128)S(1)}, f32[8,128]{1,0:T(8,128)S(1)}, f32[8,128]{1,0:T(8,128)S(1)}, f32[8,128]{1,0:T(8,128)S(1)}, f32[8,128]{1,0:T(8,128)S(1)}, /*index=5*/f32[8,128]{1,0:T(8,128)S(1)}) fusion(f32[8,128]{1,0:T(8,128)S(1)} %bitcast.449, f32[8,128]{1,0:T(8,128)S(1)} %bitcast.469, f32[8,128]{1,0:T(8,128)S(1)} %bitcast.447, ...), kind=kOutput, calls=%fused_computation.90.clone.1 | convolution fusion | flops 30682112 | bytes 131072 | tf_op jit(solution)/shard_map/while/body/eval_jaxpr/bil,bjl->bij/dot_general | solution.py:53
  80.8 1.5 scatter-add.54
  82.3 1.9 add_select_fusion.1
  86.1 2.5 %collective-permute-start.3 = (f32[3,3,1,128]{3,2,1,0:T(1,128)S(1)}, f32[3,3,1,128]{3,2,1,0:T(1,128)S(1)}, u32[]{:S(2)}, u32[]{:S(2)}) collective-permute-start(f32[3,3,1,128]{3,2,1,0:T(1,128)S(1)} %get-tuple-element.672), channel_id=1, source_target_pairs={{1,0},{2,1},{3,2},{5,4},{6,5},{7,6},{9,8},{10,9},{11,10},{13,12},{... | collective-permute-start | bytes 13832 | tf_op jit(solution)/shard_map/ppermute | solution.py:31
  88.6 3.4 %collective-permute-start.4 = (f32[3,3,1,128]{3,2,1,0:T(1,128)S(1)}, f32[3,3,1,128]{3,2,1,0:T(1,128)S(1)}, u32[]{:S(2)}, u32[]{:S(2)}) collective-permute-start(f32[3,3,1,128]{3,2,1,0:T(1,128)S(1)} %get-tuple-element.671), channel_id=1, source_target_pairs={{0,1},{1,2},{2,3},{4,5},{5,6},{6,7},{8,9},{9,10},{10,11},{12,13},{... | collective-permute-start | bytes 13832 | tf_op jit(solution)/shard_map/ppermute | solution.py:31
  92.1 2.0 %collective-permute-done.4 = f32[3,3,1,128]{3,2,1,0:T(1,128)S(1)} collective-permute-done((f32[3,3,1,128]{3,2,1,0:T(1,128)S(1)}, f32[3,3,1,128]{3,2,1,0:T(1,128)S(1)}, u32[]{:S(2)}, u32[]{:S(2)}) %collective-permute-start.4) | collective-permute-done | bytes 4640 | tf_op jit(solution)/shard_map/ppermute | solution.py:31
  94.2 1.9 collective-permute-start.5
  96.1 11.4 %collective-permute-done.5 = f32[3,1,16,128]{3,2,1,0:T(8,128)S(1)} collective-permute-done((f32[3,1,16,128]{3,2,1,0:T(8,128)S(1)}, f32[3,1,16,128]{3,2,1,0:T(8,128)S(1)}, u32[]{:S(2)}, u32[]{:S(2)}) %collective-permute-start.5) | collective-permute-done | bytes 24608 | tf_op jit(solution)/shard_map/ppermute | solution.py:37
  107.6 1.9 collective-permute-start.6
  109.5 1.7 collective-permute-done.6
  111.2 3.6 %collective-permute-start.7 = (f32[5,3,1,128]{3,2,1,0:T(1,128)S(1)}, f32[5,3,1,128]{3,2,1,0:T(1,128)S(1)}, u32[]{:S(2)}, u32[]{:S(2)}) collective-permute-start(f32[5,3,1,128]{3,2,1,0:T(1,128)S(1)} %get-tuple-element.665), channel_id=1, source_target_pairs={{0,1},{1,2},{2,3},{4,5},{5,6},{6,7},{8,9},{9,10},{10,11},{12,13},{... | collective-permute-start | bytes 23048 | tf_op jit(solution)/shard_map/ppermute | solution.py:20
  114.8 2.2 %collective-permute-start.8 = (f32[5,3,1,128]{3,2,1,0:T(1,128)S(1)}, f32[5,3,1,128]{3,2,1,0:T(1,128)S(1)}, u32[]{:S(2)}, u32[]{:S(2)}) collective-permute-start(f32[5,3,1,128]{3,2,1,0:T(1,128)S(1)} %get-tuple-element.666), channel_id=1, source_target_pairs={{1,0},{2,1},{3,2},{5,4},{6,5},{7,6},{9,8},{10,9},{11,10},{13,12},{... | collective-permute-start | bytes 23048 | tf_op jit(solution)/shard_map/ppermute | solution.py:23
  117.0 3.3 %collective-permute-done.8 = f32[5,3,1,128]{3,2,1,0:T(1,128)S(1)} collective-permute-done((f32[5,3,1,128]{3,2,1,0:T(1,128)S(1)}, f32[5,3,1,128]{3,2,1,0:T(1,128)S(1)}, u32[]{:S(2)}, u32[]{:S(2)}) %collective-permute-start.8) | collective-permute-done | bytes 7712 | tf_op jit(solution)/shard_map/ppermute | solution.py:23
  120.5 49.1 %while.47 = (s32[]{:T(128)}, f32[4,3,2,4,128]{4,3,2,1,0:T(4,128)S(1)}, f32[4,4,3,2,4,128]{5,4,3,2,1,0:T(4,128)S(1)}, s32[4]{0:T(128)S(1)}, s32[2,16,2,16]{3,1,0,...) while((s32[]{:T(128)}, ...), condition=%wide.region_58.59_spmd, body=%wide.region_30.58_spmd.sunk | while | flops 162505744 | bytes 6986204 | solution.py:146
  122.0 1.5 fusion.225
  123.5 1.5 fusion.224
  124.9 1.5 fusion.223
  127.1 3.5 %fusion.227 = (f32[8,128]{1,0:T(8,128)S(1)}, f32[8,128]{1,0:T(8,128)S(1)}, f32[8,128]{1,0:T(8,128)S(1)}, f32[8,128]{1,0:T(8,128)S(1)}, f32[8,128]{1,0:T(8,128)S(...) fusion(f32[8,128]{1,0:T(8,128)S(1)} %bitcast.493, ...), kind=kOutput, calls=%fused_computation.192.clone.1 | convolution fusion | flops 35647488 | bytes 2834432 | tf_op jit(solution)/shard_map/while/body/eval_jaxpr/bil,bjl->bij/dot_general | solution.py:53
  130.6 2.1 %fusion.228 = (f32[8,128]{1,0:T(8,128)S(1)}, f32[8,128]{1,0:T(8,128)S(1)}, f32[8,128]{1,0:T(8,128)S(1)}, f32[8,128]{1,0:T(8,128)S(1)}, f32[8,128]{1,0:T(8,128)S(1)}, /*index=5*/f32[8,128]{1,0:T(8,128)S(1)}) fusion(f32[8,128]{1,0:T(8,128)S(1)} %bitcast.474, f32[8,128]{1,0:T(8,128)S(1)} %bitcast.494, f32[8,128]{1,0:T(8,128)S(1)} %bitcast.472, ...), kind=kOutput, calls=%fused_computation.241.clone.1 | convolution fusion | flops 30682112 | bytes 131072 | tf_op jit(solution)/shard_map/while/body/eval_jaxpr/bil,bjl->bij/dot_general | solution.py:53
  134.3 1.5 fusion.225
  135.8 1.5 fusion.224
  137.2 1.5 fusion.223
  139.3 3.5 %fusion.227 = (f32[8,128]{1,0:T(8,128)S(1)}, f32[8,128]{1,0:T(8,128)S(1)}, f32[8,128]{1,0:T(8,128)S(1)}, f32[8,128]{1,0:T(8,128)S(1)}, f32[8,128]{1,0:T(8,128)S(...) fusion(f32[8,128]{1,0:T(8,128)S(1)} %bitcast.493, ...), kind=kOutput, calls=%fused_computation.192.clone.1 | convolution fusion | flops 35647488 | bytes 2834432 | tf_op jit(solution)/shard_map/while/body/eval_jaxpr/bil,bjl->bij/dot_general | solution.py:53
  142.9 2.1 %fusion.228 = (f32[8,128]{1,0:T(8,128)S(1)}, f32[8,128]{1,0:T(8,128)S(1)}, f32[8,128]{1,0:T(8,128)S(1)}, f32[8,128]{1,0:T(8,128)S(1)}, f32[8,128]{1,0:T(8,128)S(1)}, /*index=5*/f32[8,128]{1,0:T(8,128)S(1)}) fusion(f32[8,128]{1,0:T(8,128)S(1)} %bitcast.474, f32[8,128]{1,0:T(8,128)S(1)} %bitcast.494, f32[8,128]{1,0:T(8,128)S(1)} %bitcast.472, ...), kind=kOutput, calls=%fused_computation.241.clone.1 | convolution fusion | flops 30682112 | bytes 131072 | tf_op jit(solution)/shard_map/while/body/eval_jaxpr/bil,bjl->bij/dot_general | solution.py:53
  146.6 1.5 fusion.225
  148.0 1.5 fusion.224
  149.5 1.5 fusion.223
  151.6 3.5 %fusion.227 = (f32[8,128]{1,0:T(8,128)S(1)}, f32[8,128]{1,0:T(8,128)S(1)}, f32[8,128]{1,0:T(8,128)S(1)}, f32[8,128]{1,0:T(8,128)S(1)}, f32[8,128]{1,0:T(8,128)S(...) fusion(f32[8,128]{1,0:T(8,128)S(1)} %bitcast.493, ...), kind=kOutput, calls=%fused_computation.192.clone.1 | convolution fusion | flops 35647488 | bytes 2834432 | tf_op jit(solution)/shard_map/while/body/eval_jaxpr/bil,bjl->bij/dot_general | solution.py:53
  155.1 2.1 %fusion.228 = (f32[8,128]{1,0:T(8,128)S(1)}, f32[8,128]{1,0:T(8,128)S(1)}, f32[8,128]{1,0:T(8,128)S(1)}, f32[8,128]{1,0:T(8,128)S(1)}, f32[8,128]{1,0:T(8,128)S(1)}, /*index=5*/f32[8,128]{1,0:T(8,128)S(1)}) fusion(f32[8,128]{1,0:T(8,128)S(1)} %bitcast.474, f32[8,128]{1,0:T(8,128)S(1)} %bitcast.494, f32[8,128]{1,0:T(8,128)S(1)} %bitcast.472, ...), kind=kOutput, calls=%fused_computation.241.clone.1 | convolution fusion | flops 30682112 | bytes 131072 | tf_op jit(solution)/shard_map/while/body/eval_jaxpr/bil,bjl->bij/dot_general | solution.py:53
  158.9 1.5 fusion.225
  160.3 1.5 fusion.224
  161.8 1.5 fusion.223
  163.9 3.5 %fusion.227 = (f32[8,128]{1,0:T(8,128)S(1)}, f32[8,128]{1,0:T(8,128)S(1)}, f32[8,128]{1,0:T(8,128)S(1)}, f32[8,128]{1,0:T(8,128)S(1)}, f32[8,128]{1,0:T(8,128)S(...) fusion(f32[8,128]{1,0:T(8,128)S(1)} %bitcast.493, ...), kind=kOutput, calls=%fused_computation.192.clone.1 | convolution fusion | flops 35647488 | bytes 2834432 | tf_op jit(solution)/shard_map/while/body/eval_jaxpr/bil,bjl->bij/dot_general | solution.py:53
  167.4 2.1 %fusion.228 = (f32[8,128]{1,0:T(8,128)S(1)}, f32[8,128]{1,0:T(8,128)S(1)}, f32[8,128]{1,0:T(8,128)S(1)}, f32[8,128]{1,0:T(8,128)S(1)}, f32[8,128]{1,0:T(8,128)S(1)}, /*index=5*/f32[8,128]{1,0:T(8,128)S(1)}) fusion(f32[8,128]{1,0:T(8,128)S(1)} %bitcast.474, f32[8,128]{1,0:T(8,128)S(1)} %bitcast.494, f32[8,128]{1,0:T(8,128)S(1)} %bitcast.472, ...), kind=kOutput, calls=%fused_computation.241.clone.1 | convolution fusion | flops 30682112 | bytes 131072 | tf_op jit(solution)/shard_map/while/body/eval_jaxpr/bil,bjl->bij/dot_general | solution.py:53
  169.7 1.5 scatter-add.66
  171.1 1.9 add_select_fusion
  175.0 2.2 %collective-permute-start.9 = (f32[3,3,1,128]{3,2,1,0:T(1,128)S(1)}, f32[3,3,1,128]{3,2,1,0:T(1,128)S(1)}, u32[]{:S(2)}, u32[]{:S(2)}) collective-permute-start(f32[3,3,1,128]{3,2,1,0:T(1,128)S(1)} %get-tuple-element.670), channel_id=1, source_target_pairs={{1,0},{2,1},{3,2},{5,4},{6,5},{7,6},{9,8},{10,9},{11,10},{13,12},{... | collective-permute-start | bytes 13832 | tf_op jit(solution)/shard_map/ppermute | solution.py:31
  177.2 3.6 %collective-permute-start.10 = (f32[3,3,1,128]{3,2,1,0:T(1,128)S(1)}, f32[3,3,1,128]{3,2,1,0:T(1,128)S(1)}, u32[]{:S(2)}, u32[]{:S(2)}) collective-permute-start(f32[3,3,1,128]{3,2,1,0:T(1,128)S(1)} %get-tuple-element.669), channel_id=1, source_target_pairs={{0,1},{1,2},{2,3},{4,5},{5,6},{6,7},{8,9},{9,10},{10,11},{12,13},{... | collective-permute-start | bytes 13832 | tf_op jit(solution)/shard_map/ppermute | solution.py:31
  180.9 1.8 collective-permute-done.10
  182.8 1.9 collective-permute-start.11
  184.7 11.3 %collective-permute-done.11 = f32[3,1,16,128]{3,2,1,0:T(8,128)S(1)} collective-permute-done((f32[3,1,16,128]{3,2,1,0:T(8,128)S(1)}, f32[3,1,16,128]{3,2,1,0:T(8,128)S(1)}, u32[]{:S(2)}, u32[]{:S(2)}) %collective-permute-start.11) | collective-permute-done | bytes 24608 | tf_op jit(solution)/shard_map/ppermute | solution.py:37
  (182 shorter events, 23.9 us)
Async XLA Ops:
  0.6 0.8 copy-start.7
  0.6 0.8 copy-start.6
  0.7 0.9 copy-start.1
  2.4 18.2 %copy-start.4 = (f32[16,16]{1,0:T(8,128)S(1)}, f32[16,16]{1,0:T(8,128)}, u32[]{:S(2)}) copy-start(f32[16,16]{1,0:T(8,128)} %param.51) | copy-start | bytes 3076
  2.4 20.4 %collective-permute-start = (f32[5,1,16,128]{3,2,1,0:T(8,128)S(1)}, f32[5,1,16,128]{3,2,1,0:T(8,128)S(1)}, u32[]{:S(2)}, u32[]{:S(2)}) collective-permute-start(f32[5,1,16,128]{3,2,1,0:T(8,128)S(1)} %pad_maximum_fusion.9), channel_id=1, source_target_pairs={{4,0},{8,4},{12,8},{16,12},{20,16},{24,20},{28,24},{32,28},{36,32}... | collective-permute-start | bytes 122888 | tf_op jit(solution)/shard_map/ppermute | solution.py:37
  20.7 0.7 copy-start.8
  22.8 6.5 %copy-start.5 = (s32[2,16,2,16]{3,2,1,0:T(2,128)S(1)}, s32[2,16,2,16]{3,2,1,0:T(2,128)}, u32[]{:S(2)}) copy-start(s32[2,16,2,16]{3,2,1,0:T(2,128)} %param.50) | copy-start | bytes 12292
  22.8 6.5 %collective-permute-start.1 = (f32[5,3,1,128]{3,2,1,0:T(1,128)S(1)}, f32[5,3,1,128]{3,2,1,0:T(1,128)S(1)}, u32[]{:S(2)}, u32[]{:S(2)}) collective-permute-start(f32[5,3,1,128]{3,2,1,0:T(1,128)S(1)} %get-tuple-element.667), channel_id=1, source_target_pairs={{0,1},{1,2},{2,3},{4,5},{5,6},{6,7},{8,9},{9,10},{10,11},{12,13},{... | collective-permute-start | bytes 23048 | tf_op jit(solution)/shard_map/ppermute | solution.py:20
  26.2 5.5 %collective-permute-start.2 = (f32[5,3,1,128]{3,2,1,0:T(1,128)S(1)}, f32[5,3,1,128]{3,2,1,0:T(1,128)S(1)}, u32[]{:S(2)}, u32[]{:S(2)}) collective-permute-start(f32[5,3,1,128]{3,2,1,0:T(1,128)S(1)} %get-tuple-element.668), channel_id=1, source_target_pairs={{1,0},{2,1},{3,2},{5,4},{6,5},{7,6},{9,8},{10,9},{11,10},{13,12},{... | collective-permute-start | bytes 23048 | tf_op jit(solution)/shard_map/ppermute | solution.py:23
  86.1 5.9 %collective-permute-start.3 = (f32[3,3,1,128]{3,2,1,0:T(1,128)S(1)}, f32[3,3,1,128]{3,2,1,0:T(1,128)S(1)}, u32[]{:S(2)}, u32[]{:S(2)}) collective-permute-start(f32[3,3,1,128]{3,2,1,0:T(1,128)S(1)} %get-tuple-element.672), channel_id=1, source_target_pairs={{1,0},{2,1},{3,2},{5,4},{6,5},{7,6},{9,8},{10,9},{11,10},{13,12},{... | collective-permute-start | bytes 13832 | tf_op jit(solution)/shard_map/ppermute | solution.py:31
  88.6 5.5 %collective-permute-start.4 = (f32[3,3,1,128]{3,2,1,0:T(1,128)S(1)}, f32[3,3,1,128]{3,2,1,0:T(1,128)S(1)}, u32[]{:S(2)}, u32[]{:S(2)}) collective-permute-start(f32[3,3,1,128]{3,2,1,0:T(1,128)S(1)} %get-tuple-element.671), channel_id=1, source_target_pairs={{0,1},{1,2},{2,3},{4,5},{5,6},{6,7},{8,9},{9,10},{10,11},{12,13},{... | collective-permute-start | bytes 13832 | tf_op jit(solution)/shard_map/ppermute | solution.py:31
  94.2 13.3 %collective-permute-start.5 = (f32[3,1,16,128]{3,2,1,0:T(8,128)S(1)}, f32[3,1,16,128]{3,2,1,0:T(8,128)S(1)}, u32[]{:S(2)}, u32[]{:S(2)}) collective-permute-start(f32[3,1,16,128]{3,2,1,0:T(8,128)S(1)} %slice.1180), channel_id=1, source_target_pairs={{764,0},{0,4},{4,8},{8,12},{12,16},{16,20},{20,24},{24,28},{28,32}... | collective-permute-start | bytes 73736 | tf_op jit(solution)/shard_map/ppermute | solution.py:37
  96.1 11.4 %copy-start.2 = (f32[3,2,16,128]{3,2,1,0:T(8,128)S(1)}, f32[3,2,16,128]{3,2,1,0:T(8,128)}, u32[]{:S(2)}) copy-start(f32[3,2,16,128]{3,2,1,0:T(8,128)} %param.46) | copy-start | bytes 147460
  107.5 12.8 %copy-start = (f32[3,2,16,128]{3,2,1,0:T(8,128)}, f32[3,2,16,128]{3,2,1,0:T(8,128)S(1)}, u32[]{:S(2)}) copy-start(f32[3,2,16,128]{3,2,1,0:T(8,128)S(1)} %multiply_add_fusion.1) | copy-start | bytes 147460
  107.6 3.6 %collective-permute-start.6 = (f32[5,1,16,128]{3,2,1,0:T(8,128)S(1)}, f32[5,1,16,128]{3,2,1,0:T(8,128)S(1)}, u32[]{:S(2)}, u32[]{:S(2)}) collective-permute-start(f32[5,1,16,128]{3,2,1,0:T(8,128)S(1)} %pad_maximum_fusion.8), channel_id=1, source_target_pairs={{4,0},{8,4},{12,8},{16,12},{20,16},{24,20},{28,24},{32,28},{36,32}... | collective-permute-start | bytes 122888 | tf_op jit(solution)/shard_map/ppermute | solution.py:37
  111.2 5.9 %collective-permute-start.7 = (f32[5,3,1,128]{3,2,1,0:T(1,128)S(1)}, f32[5,3,1,128]{3,2,1,0:T(1,128)S(1)}, u32[]{:S(2)}, u32[]{:S(2)}) collective-permute-start(f32[5,3,1,128]{3,2,1,0:T(1,128)S(1)} %get-tuple-element.665), channel_id=1, source_target_pairs={{0,1},{1,2},{2,3},{4,5},{5,6},{6,7},{8,9},{9,10},{10,11},{12,13},{... | collective-permute-start | bytes 23048 | tf_op jit(solution)/shard_map/ppermute | solution.py:20
  114.8 5.5 %collective-permute-start.8 = (f32[5,3,1,128]{3,2,1,0:T(1,128)S(1)}, f32[5,3,1,128]{3,2,1,0:T(1,128)S(1)}, u32[]{:S(2)}, u32[]{:S(2)}) collective-permute-start(f32[5,3,1,128]{3,2,1,0:T(1,128)S(1)} %get-tuple-element.666), channel_id=1, source_target_pairs={{1,0},{2,1},{3,2},{5,4},{6,5},{7,6},{9,8},{10,9},{11,10},{13,12},{... | collective-permute-start | bytes 23048 | tf_op jit(solution)/shard_map/ppermute | solution.py:23
  175.0 5.9 %collective-permute-start.9 = (f32[3,3,1,128]{3,2,1,0:T(1,128)S(1)}, f32[3,3,1,128]{3,2,1,0:T(1,128)S(1)}, u32[]{:S(2)}, u32[]{:S(2)}) collective-permute-start(f32[3,3,1,128]{3,2,1,0:T(1,128)S(1)} %get-tuple-element.670), channel_id=1, source_target_pairs={{1,0},{2,1},{3,2},{5,4},{6,5},{7,6},{9,8},{10,9},{11,10},{13,12},{... | collective-permute-start | bytes 13832 | tf_op jit(solution)/shard_map/ppermute | solution.py:31
  177.2 5.5 %collective-permute-start.10 = (f32[3,3,1,128]{3,2,1,0:T(1,128)S(1)}, f32[3,3,1,128]{3,2,1,0:T(1,128)S(1)}, u32[]{:S(2)}, u32[]{:S(2)}) collective-permute-start(f32[3,3,1,128]{3,2,1,0:T(1,128)S(1)} %get-tuple-element.669), channel_id=1, source_target_pairs={{0,1},{1,2},{2,3},{4,5},{5,6},{6,7},{8,9},{9,10},{10,11},{12,13},{... | collective-permute-start | bytes 13832 | tf_op jit(solution)/shard_map/ppermute | solution.py:31
  182.8 13.3 %collective-permute-start.11 = (f32[3,1,16,128]{3,2,1,0:T(8,128)S(1)}, f32[3,1,16,128]{3,2,1,0:T(8,128)S(1)}, u32[]{:S(2)}, u32[]{:S(2)}) collective-permute-start(f32[3,1,16,128]{3,2,1,0:T(8,128)S(1)} %slice.1196), channel_id=1, source_target_pairs={{764,0},{0,4},{4,8},{8,12},{12,16},{16,20},{20,24},{24,28},{28,32}... | collective-permute-start | bytes 73736 | tf_op jit(solution)/shard_map/ppermute | solution.py:37
  196.1 0.7 copy-start.3
where the time goes:
time: 198 us; the launch traced here: 197 us
  matrix products  83.8 us (42%)
  starting transfers between devices  47.3 us (24%)
  waiting for transfers between devices  33.9 us (17%)
  local copies, waits for them, and re-layouts  16.5 us (8%)
  other arithmetic  7.77 us (4%)
  loops' own time  6.09 us (3%)
    dot_general x40, matrix products, soft_table(): jnp.einsum('bil,bjl->bij', by_rows, hot_other, precision=lax.Precision.HI...  79 us
    ppermute x4, waiting for transfers between devices, shifted(): return lax.ppermute(block, axis, route)  24.3 us
    ppermute x4, starting transfers between devices, shifted(): return lax.ppermute(block, axis, route)  24 us
    ppermute x4, starting transfers between devices, from_behind(): lax.ppermute(value, axis, [(source, source + steps) for source in range(f...  11.7 us
    ppermute x2, starting transfers between devices, extended_2(): lax.ppermute(lax.slice_in_dim(block, block.shape[dim] - width, None, axis...  7.02 us
    another operation x2, loops' own time, block_forces(): results = lax.map(one_block, jnp.arange(blocks, dtype=jnp.int32))  6.09 us
    ppermute x2, waiting for transfers between devices, extended_2(): lax.ppermute(lax.slice_in_dim(block, 0, width, axis=dim), axis, backward)  5.71 us
    dynamic_slice x8, local copies, waits for them, and re-layouts, block_forces(): results = lax.map(one_block, jnp.arange(blocks, dtype=jnp.int32))  4.81 us
  transfers between devices with their start and end apart: 12, of which 7 were waited for; matrix products, arithmetic and copies ran while one was open for 1% of the time, Pallas kernels for 0%

commit v1 on v0

v1 whole, which is shorter than its diff:
```python
import functools

import jax
import jax.numpy as jnp
from jax import lax
from jax.experimental import pallas as pl
from jax.experimental.pallas import tpu as pltpu
from jax.sharding import PartitionSpec as P

DT = 0.05
CORE = 0.09
CHANNELS = 6
ROWS = 24
COLS = 4
BINS = ROWS * COLS
GROUPS = BINS // 8
RAW_A, RAW_B, RAW_W, RAW_Q = 0, 32, 96, 112
RAW = 120
BF = jnp.bfloat16
F32 = jnp.float32


def split3(value):
    high = value.astype(BF).astype(F32)
    rest = value - high
    mid = rest.astype(BF).astype(F32)
    return high, mid, rest - mid


def force_kernel(
    step, parity, own, near, far, vel, repulsion, *refs
):
    outs, (pos, raw, a_ref, b_ref, w_ref, acc, ut, qi, sh) = refs[:3], refs[3:]
    swap = parity[0] == 1
    zero = jnp.zeros((8, 128), F32)
    one = jnp.ones((8, 128), F32)

    def put(base, group, value):
        raw[pl.ds(group * 8 * RAW + base, 8, stride=RAW), :] = value

    per_col = ROWS // 8
    for group in range(GROUPS):
        col, inner = divmod(group, per_col)
        at = slice(inner * 8, inner * 8 + 8)
        if col in (1, 2):
            fields = [own[c, col - 1, at, :] for c in range(CHANNELS)]
        else:
            first, second = (far, near) if col == 0 else (near, far)
            fields = [jnp.where(swap, second[c, at, :], first[c, at, :]) for c in range(CHANNELS)]
        x, y, z, charge, code, names = fields
        x = x + (col - 1.5)
        for c, value in enumerate((x, y, z, charge, code)):
            pos[c, group * 8 : group * 8 + 8, :] = value
        for k, coord in enumerate((x, y, z)):
            h, m, l = split3(coord)
            base = RAW_A + (0, 6, 22)[k]
            for i, value in enumerate((h, h, m, h, l, m)):
                put(base + i, group, 2 * value)
            if k < 2:
                for i, value in enumerate((h, m, h, l, h, m)):
                    put(RAW_B + 6 * k + i, group, value)
            for i, value in enumerate((h, m, l)):
                put(RAW_W + 4 * i + k, group, value)
        flat = x * x + y * y
        for i, value in enumerate(split3(-(flat + z * z))):
            put(RAW_A + 16 + i, group, one)
            put(RAW_A + 19 + i, group, value)
        for v, shift in enumerate((-1.0, 0.0, 1.0)):
            other = z + shift
            base = RAW_B + 16 + 16 * v
            for i, value in enumerate(split3((1.0 - flat) - other * other)):
                put(base + i, group, value)
                put(base + 3 + i, group, one)
            h, m, l = split3(other)
            for i, value in enumerate((h, m, h, l, h, m)):
                put(base + 6 + i, group, value)
            for i in range(12, 16):
                put(base + i, group, zero)
        for i in range(12, 16):
            put(RAW_A + i, group, zero)
            put(RAW_A + 16 + i, group, zero)
            put(RAW_B + i, group, zero)
            put(RAW_W + i, group, zero)
        put(RAW_W + 3, group, one)
        put(RAW_W + 7, group, zero)
        put(RAW_W + 11, group, zero)
        for i, value in enumerate(split3(charge)):
            put(RAW_Q + i, group, value)
        put(RAW_Q + 3, group, names)
        for i in range(4, 8):
            put(RAW_Q + i, group, zero)

    code_rows = lax.broadcasted_iota(jnp.int32, (16, 128), 0).astype(F32) + 1.0
    table = 0.5 * (repulsion[...] + repulsion[...].T)
    table = jnp.concatenate(split3(table), axis=0).astype(BF)
    half_tile = jnp.zeros((8, 128), F32)

    def convert(b, carry):
        base = pl.multiple_of(b * RAW, 8)
        a_ref[b, 0:32, :] = raw[pl.ds(base + RAW_A, 32), :].astype(BF)
        b_ref[b, 0:64, :] = raw[pl.ds(base + RAW_B, 64), :].astype(BF)
        w_ref[b] = raw[pl.ds(base + RAW_W, 16), :].astype(BF)
        a_ref[b, 80:96, :] = jnp.concatenate([raw[pl.ds(base + RAW_Q, 8), :], half_tile], 0).astype(BF)
        hot = (pos[4, pl.ds(b, 1), :] == code_rows).astype(F32).astype(BF)
        b_ref[b, 64:80, :] = hot
        a_ref[b, 32:80, :] = jnp.dot(table, hot, preferred_element_type=F32).astype(BF)
        return carry

    lax.fori_loop(0, BINS, convert, 0, unroll=4)

    acc[...] = jnp.zeros_like(acc)
    row16 = lax.broadcasted_iota(jnp.int32, (16, 128), 0)
    spread = jnp.where(row16 < 3, 1.0, 0.0).astype(BF)
    spread_names = jnp.where(row16 == 3, 1.0, 0.0).astype(BF)
    slot = lax.broadcasted_iota(jnp.int32, (16, 128), 1).astype(F32)
    tilt = {0: None}
    for dz in (-1, 1):
        tilt[dz] = jnp.where(row16 == 12, float(dz), 0.0).astype(BF)
    zero_d = jnp.zeros((32, 128), BF)
    zero_t = jnp.zeros((48, 128), BF)

    def weights(b, dz):
        w = w_ref[b]
        if dz:
            w = w + tilt[dz]
        return jnp.concatenate([w, w], 1)

    def sweep(total, bin_of, pairs):
        ut[...] = jnp.zeros_like(ut)
        qi[...] = jnp.zeros_like(qi)
        sh[...] = jnp.zeros_like(sh)

        def reduce_stage(b):
            lhs, rhs = [], []
            for k, (offset, dz) in enumerate(pairs):
                both = sh[k]
                if offset and len(pairs) > 3:
                    lhs.append(weights(b + offset, dz))
                    rhs.append(both)
                stacked = jnp.concatenate([both[:, :128], both[:, 128:]], 0)
                acc[b + offset] += jnp.dot(weights(b, -dz), stacked, preferred_element_type=F32)
            if lhs:
                acc[b] += lax.dot_general(
                    jnp.concatenate(lhs, 1), jnp.concatenate(rhs, 1), (((1,), (1,)), ((), ())), preferred_element_type=F32
                )

        def scalar_stage(b):
            for k, (offset, dz) in enumerate(pairs):
                other = pos[3, pl.ds(b + offset, 1), :]
                for i in range(0, 128, 16):
                    reach = ut[k, i : i + 16, :128]
                    inside = jnp.maximum(reach, 0.0)
                    inverse = lax.rsqrt((1.0 + CORE) - reach)
                    coulomb = (qi[i : i + 16, :] * other) * inside * (inverse * inverse * inverse)
                    scalar = (ut[k, i : i + 16, 128:] + coulomb) * inside
                    high = scalar.astype(BF)
                    sh[k, i : i + 16, :128] = high
                    sh[k, i : i + 16, 128:] = (scalar - high.astype(F32)).astype(BF)

        def product_stage(b):
            a = a_ref[b].T
            for k, (offset, dz) in enumerate(pairs):
                other = b + offset
                b_dist = jnp.concatenate(
                    [b_ref[other, 0:16, :], b_ref[other, 32 + 16 * dz : 48 + 16 * dz, :]], axis=0
                )
                hot = b_ref[other, 64:80, :]
                left = [jnp.concatenate([b_dist, zero_t], 0)]
                right = jnp.concatenate([zero_d, hot, hot, hot], 0)
                lhs = a[:, 0:80]
                if not offset:
                    names = lax.dot_general(
                        a_ref[b, 80:96, :], spread_names, (((0,), (0,)), ((), ())), preferred_element_type=F32
                    )
                    first = (names[0:16, :] == slot).astype(F32)
                    second = (names[16:32, :] == slot).astype(F32)
                    drop = jnp.concatenate([first, second], 0)
                    again = jnp.concatenate([second, first], 0).astype(BF)
                    out = jnp.dot(lhs, jnp.concatenate([left[0], right], 1), preferred_element_type=F32)
                    hits = lax.dot_general(
                        drop.astype(BF), again, (((0,), (0,)), ((), ())), preferred_element_type=F32
                    )
                    ut[k, :, :128] = jnp.where(hits > 0.0, -1.0, out[:, :128])
                    ut[k, :, 128:] = out[:, 128:]
                else:
                    ut[k] = jnp.dot(lhs, jnp.concatenate([left[0], right], 1), preferred_element_type=F32)
            qi[...] = jnp.dot(a[:, 80:96], spread, preferred_element_type=F32)

        def body(n, carry):
            reduce_stage(bin_of(jnp.maximum(n - 2, 0)))
            scalar_stage(bin_of(jnp.clip(n - 1, 0, total - 1)))
            product_stage(bin_of(jnp.minimum(n, total - 1)))
            return carry

        lax.fori_loop(0, total + 2, body, 0)

    ahead = tuple((ROWS + dz, dz) for dz in (-1, 0, 1))
    sweep(18, lambda n: n + 1, ahead)
    sweep(36, lambda n: ROWS + 1 + n + (n // 18) * (ROWS - 18), ((0, 0), (1, 1)) + ahead)

    acc_flat = acc.reshape(BINS * 16, 128)
    for group in range(per_col, 3 * per_col):
        col, inner = divmod(group, per_col)
        at = slice(inner * 8, inner * 8 + 8)

        def take(k):
            return acc_flat[pl.ds(group * 128 + k, 8, stride=16), :]

        count = take(3)
        for c in range(3):
            here = pos[c, group * 8 : group * 8 + 8, :]
            back = (take(c) + take(4 + c)) + take(8 + c)
            if c == 2:
                back = back + take(12)
            force = here * count - back
            v = vel[c, col - 1, at, :] + 0.5 * DT * force
            if step == 0:
                v = v + 0.5 * DT * force
                outs[0][c, col - 1, at, :] = own[c, col - 1, at, :] + DT * v
            else:
                outs[0][c, col - 1, at, :] = own[c, col - 1, at, :]
                outs[2][c, col - 1, at, :] = force
            outs[1][c, col - 1, at, :] = v
    if step == 0:
        outs[2][...] = jnp.zeros_like(outs[2])


def forces_call(step, parity, own, near, far, vel, repulsion):
    out = jax.ShapeDtypeStruct((3, 2, ROWS, 128), F32)
    vmem = pl.BlockSpec(memory_space=pltpu.VMEM)
    return pl.pallas_call(
        functools.partial(force_kernel, step),
        out_shape=(out, out, out),
        in_specs=[pl.BlockSpec(memory_space=pltpu.SMEM), vmem, vmem, vmem, vmem, vmem],
        out_specs=(vmem, vmem, vmem),
        scratch_shapes=[
            pltpu.VMEM((5, BINS, 128), F32),
            pltpu.VMEM((BINS * RAW, 128), F32),
            pltpu.VMEM((BINS, 96, 128), BF),
            pltpu.VMEM((BINS, 80, 128), BF),
            pltpu.VMEM((BINS, 16, 128), BF),
            pltpu.VMEM((BINS, 16, 128), F32),
            pltpu.VMEM((5, 128, 256), F32),
            pltpu.VMEM((128, 128), F32),
            pltpu.VMEM((5, 128, 256), BF),
        ],
        compiler_params=pltpu.CompilerParams(vmem_limit_bytes=56 * 1024 * 1024),
        name=f"forces{step}",
    )(parity, own, near, far, vel, repulsion)


def swap_pairs(value, odd):
    count = lax.axis_size("gx")
    start = 1 if odd else 0
    route = []
    for i in range(start, count + start, 2):
        a, b = i % count, (i + 1) % count
        route += [(a, b), (b, a)]
    return lax.ppermute(value, "gx", route)


def with_rows(block):
    count = lax.axis_size("gz")
    up = [(i, i + 1) for i in range(count - 1)]
    down = [(b, a) for a, b in up]
    low = lax.ppermute(block[:, :, 17:18], "gz", up)
    high = lax.ppermute(block[:, :, 2:3], "gz", down)
    row = lax.broadcasted_iota(jnp.int32, (1, 1, ROWS, 1), 2)
    return jnp.where(row == 1, low, jnp.where(row == 18, high, block))


def exchanged(block, parity):
    own = with_rows(block)
    far = swap_pairs(jnp.where(parity == 1, own[:, 1], own[:, 0]), True)
    near = swap_pairs(jnp.where(parity == 1, own[:, 0], own[:, 1]), False)
    return own, near, far


def local(positions, velocities, forces, charge, atom_type, bin_count, exclusions, repulsion):
    columns, depth, slots = positions.shape[1:]
    velocities = velocities + 0.5 * DT * forces
    positions = positions + DT * velocities
    slot_ids = jnp.arange(slots, dtype=jnp.int32)
    live = slot_ids < bin_count[..., None]
    code = jnp.where(live, atom_type + 1, 0).astype(F32)
    live_charge = jnp.where(live, charge, 0.0)
    names = exclusions.reshape(columns, depth, -1).astype(F32)
    names = jnp.pad(names, ((0, 0), (0, 0), (0, slots - names.shape[-1])))
    packed = jnp.concatenate([positions, live_charge[None], code[None], names[None]], axis=0)
    place = ((0, 0), (0, 0), (2, ROWS - 2 - depth), (0, 0))
    packed = jnp.pad(packed, place)
    half = jnp.pad(velocities, place)
    parity = lax.axis_index("gx") % 2
    flag = parity.astype(jnp.int32).reshape(1)
    own, near, far = exchanged(packed, parity)
    p, v, _ = forces_call(0, flag, own, near, far, half, repulsion)
    p, near_p, far_p = exchanged(p, parity)
    own = jnp.concatenate([p, own[3:]], 0)
    near = jnp.concatenate([near_p, near[3:]], 0)
    far = jnp.concatenate([far_p, far[3:]], 0)
    outs = forces_call(1, flag, own, near, far, v, repulsion)
    return tuple(o[:, :, 2 : 2 + depth] for o in outs)


def solution(mesh):
    grid = P(None, "gx", "gz", None)
    return jax.shard_map(
        local,
        mesh=mesh,
        in_specs=(
            grid, grid, grid,
            P("gx", "gz", None), P("gx", "gz", None), P("gx", "gz"), P("gx", "gz", None, None), P(),
        ),
        out_specs=(grid, grid, grid),
        check_vma=False,
    )
```

time: 198 us -> 126 us (0.64)
  matrix products: 83.8 us -> 0 us
  Pallas kernels: 0 us -> 62.2 us
  waiting for transfers between devices: 33.9 us -> 10.2 us
  local copies, waits for them, and re-layouts: 16.5 us -> 7.24 us
  loops' own time: 6.09 us -> 0 us
  other arithmetic: 7.77 us -> 2.44 us
  starting transfers between devices: 47.3 us -> 42.5 us
    dot_general x56 -> x0, matrix products: 83.8 us -> none  [the longest x40 79 us: soft_table(): jnp.einsum('bil,bjl->bij', by_rows, hot_other, precision=lax.Precision.HI...]
    pallas_call x0 -> x2, Pallas kernels: none -> 62.2 us  [forces_call(): pl.pallas_call(functools.partial(force_kernel, step), out_shape=(out, out...]
    ppermute x12 -> x8, waiting for transfers between devices: 33.9 us -> 10.2 us  [the longest x4 5.19 us: swap_pairs(): return lax.ppermute(value, 'gx', route)]
    scatter-add x12 -> x0, local copies, waits for them, and re-layouts: 6.67 us -> none  [the longest x2 2.92 us: local(): on_ext = on_ext.at[:, :columns, 1:bin_depth + 1].add(summed)]
    another operation x2 -> x0, loops' own time: 6.09 us -> none  [block_forces(): results = lax.map(one_block, jnp.arange(blocks, dtype=jnp.int32))]
    dynamic_slice x16 -> x0, local copies, waits for them, and re-layouts: 4.9 us -> none  [the longest x8 4.81 us: block_forces(): results = lax.map(one_block, jnp.arange(blocks, dtype=jnp.int32))]
    ppermute x12 -> x8, starting transfers between devices: 47.3 us -> 42.5 us  [the longest x4 24.2 us: swap_pairs(): return lax.ppermute(value, 'gx', route)]
    another operation x4 -> x0, other arithmetic: 4.53 us -> none
  transfers between devices with their start and end apart: 12 -> 8, of which waited for: 7 -> 4; matrix products, arithmetic and copies ran while one was open for 1% -> 2% of each run, Pallas kernels for 0% -> 0%
where the time goes in v1:
time: 126 us
  Pallas kernels  62.2 us (49%)
  starting transfers between devices  42.5 us (34%)
  waiting for transfers between devices  10.2 us (8%)
  local copies, waits for them, and re-layouts  7.24 us (6%)
  other arithmetic  2.44 us (2%)
    pallas_call x2, Pallas kernels, forces_call(): pl.pallas_call(functools.partial(force_kernel, step), out_shape=(out, out...  62.2 us
    ppermute x4, starting transfers between devices, swap_pairs(): return lax.ppermute(value, 'gx', route)  24.2 us
    ppermute x2, starting transfers between devices, with_rows(): high = lax.ppermute(block[:, :, 2:3], 'gz', down)  12.5 us
    ppermute x2, starting transfers between devices, with_rows(): low = lax.ppermute(block[:, :, 17:18], 'gz', up)  5.84 us
    ppermute x4, waiting for transfers between devices, swap_pairs(): return lax.ppermute(value, 'gx', route)  5.19 us
    ppermute x2, waiting for transfers between devices, with_rows(): low = lax.ppermute(block[:, :, 17:18], 'gz', up)  5.04 us
    slice x3, local copies, waits for them, and re-layouts, local(): return tuple((o[:, :, 2:2 + depth] for o in outs))  2.79 us
  transfers between devices with their start and end apart: 8, of which 4 were waited for; matrix products, arithmetic and copies ran while one was open for 2% of the time, Pallas kernels for 0%

profile of v1, /device:TPU:64, one launch (start us, length us, event | category | flops | bytes accessed | tf_op | source)
XLA Modules:
  0.0 125.5 jit_solution(9237093619812121239)
XLA Ops:
  0.6 0.0 copy-start.9
  0.6 0.0 copy-start.11
  0.7 0.0 copy-start.10
  0.7 0.8 convert_element_type.16
  1.5 0.0 copy-start.6
  1.5 0.1 convert_element_type.17
  1.6 0.0 copy-done.9
  1.6 0.0 copy-done.11
  1.6 0.0 copy-start.4
  1.6 0.0 copy-start.5
  1.6 0.1 convert_bitcast_fusion
  1.6 0.0 copy-done.10
  1.6 0.1 pad_bitcast_fusion
  1.7 0.5 copy-done.6
  2.3 0.1 copy-done.4
  2.4 0.0 copy-done.5
  2.4 10.5 %collective-permute-start.1 = (f32[6,2,1,128]{3,2,0,1:T(1,128)S(1)}, f32[6,2,1,128]{3,2,0,1:T(1,128)S(1)}, u32[]{:S(2)}, u32[]{:S(2)}) collective-permute-start(f32[6,2,1,128]{3,2,0,1:T(1,128)S(1)} %get-tuple-element.18), channel_id=1, source_target_pairs={{1,0},{2,1},{3,2},{5,4},{6,5},{7,6},{9,8},{10,9},{11,10},{13,12},{... | collective-permute-start | bytes 18440 | tf_op jit(solution)/shard_map/ppermute | solution.py:267
  13.0 1.9 %collective-permute-start = (f32[6,2,1,128]{3,2,0,1:T(1,128)S(1)}, f32[6,2,1,128]{3,2,0,1:T(1,128)S(1)}, u32[]{:S(2)}, u32[]{:S(2)}) collective-permute-start(f32[6,2,1,128]{3,2,0,1:T(1,128)S(1)} %get-tuple-element.17), channel_id=1, source_target_pairs={{0,1},{1,2},{2,3},{4,5},{5,6},{6,7},{8,9},{9,10},{10,11},{12,13},{... | collective-permute-start | bytes 18440 | tf_op jit(solution)/shard_map/ppermute | solution.py:266
  15.0 0.0 collective-permute-done.1
  15.0 3.5 %collective-permute-done = f32[6,2,1,128]{3,2,0,1:T(1,128)S(1)} collective-permute-done((f32[6,2,1,128]{3,2,0,1:T(1,128)S(1)}, f32[6,2,1,128]{3,2,0,1:T(1,128)S(1)}, u32[]{:S(2)}, u32[]{:S(2)}) %collective-permute-start) | collective-permute-done | bytes 6176 | tf_op jit(solution)/shard_map/ppermute | solution.py:266
  18.5 0.1 select_select_fusion
  18.6 0.0 copy-start
  18.7 1.9 %collective-permute-start.2 = (f32[6,24,128]{2,1,0:T(8,128)S(1)}, f32[6,24,128]{2,1,0:T(8,128)S(1)}, u32[]{:S(2)}, u32[]{:S(2)}) collective-permute-start(f32[6,24,128]{2,1,0:T(8,128)S(1)} %get-tuple-element.16), channel_id=1, source_target_pairs={{0,4},{4,0},{8,12},{12,8},{16,20},{20,16},{24,28},{28,24},{32,36},... | collective-permute-start | bytes 221192 | tf_op jit(solution)/shard_map/ppermute | solution.py:259
  20.6 10.8 %collective-permute-start.3 = (f32[6,24,128]{2,1,0:T(8,128)S(1)}, f32[6,24,128]{2,1,0:T(8,128)S(1)}, u32[]{:S(2)}, u32[]{:S(2)}) collective-permute-start(f32[6,24,128]{2,1,0:T(8,128)S(1)} %get-tuple-element.15), channel_id=1, source_target_pairs={{4,8},{8,4},{12,16},{16,12},{20,24},{24,20},{28,32},{32,28},{36,40... | collective-permute-start | bytes 221192 | tf_op jit(solution)/shard_map/ppermute | solution.py:259
  31.4 0.6 pad.14.clone.vel
  32.0 0.7 copy.29.own
  32.7 0.0 collective-permute-done.2.near
  32.7 0.0 copy-start.1
  32.7 1.9 %collective-permute-done.3.far = f32[6,24,128]{2,1,0:T(8,128)S(1)} collective-permute-done((f32[6,24,128]{2,1,0:T(8,128)S(1)}, f32[6,24,128]{2,1,0:T(8,128)S(1)}, u32[]{:S(2)}, u32[]{:S(2)}) %collective-permute-start.3) | collective-permute-done | bytes 73760 | tf_op jit(solution)/shard_map/ppermute | solution.py:259
  34.6 0.0 copy-start.2
  34.6 0.0 copy-done.1
  34.6 0.6 copy-done.2
  35.2 31.1 %forces0.1 = (f32[3,2,24,128]{3,2,1,0:T(8,128)}, f32[3,2,24,128]{3,2,1,0:T(8,128)}, f32[3,2,24,128]{3,2,1,0:T(8,128)}) custom-call(s32[1]{0:T(128)} %bitcast.parity, f32[6,2,24,128]{3,2,1,0:T(8,128)} %copy.29.own, f32[6,24,128]{2,1,0:T(8,128)} %copy-done.1, f32[6,24,128]{2,1,0:T(8,128)} %copy-done.2, f32[3,2,24,128]{3,2,1,0:T(8,128)} %pad.14.clone.vel, ...), custom_call_target="tpu_custom_call" | custom-call | tf_op jit(solution)/shard_map/forces0/pallas_call | solution.py:231
  66.3 0.8 fusion.2
  67.0 1.9 %collective-permute-start.5 = (f32[3,2,1,128]{3,2,1,0:T(1,128)S(1)}, f32[3,2,1,128]{3,2,1,0:T(1,128)S(1)}, u32[]{:S(2)}, u32[]{:S(2)}) collective-permute-start(f32[3,2,1,128]{3,2,1,0:T(1,128)S(1)} %get-tuple-element.22), channel_id=1, source_target_pairs={{1,0},{2,1},{3,2},{5,4},{6,5},{7,6},{9,8},{10,9},{11,10},{13,12},{... | collective-permute-start | bytes 9224 | tf_op jit(solution)/shard_map/ppermute | solution.py:267
  69.0 3.9 %collective-permute-start.4 = (f32[3,2,1,128]{3,2,1,0:T(1,128)S(1)}, f32[3,2,1,128]{3,2,1,0:T(1,128)S(1)}, u32[]{:S(2)}, u32[]{:S(2)}) collective-permute-start(f32[3,2,1,128]{3,2,1,0:T(1,128)S(1)} %get-tuple-element.21), channel_id=1, source_target_pairs={{0,1},{1,2},{2,3},{4,5},{5,6},{6,7},{8,9},{9,10},{10,11},{12,13},{... | collective-permute-start | bytes 9224 | tf_op jit(solution)/shard_map/ppermute | solution.py:266
  72.9 0.0 copy-done
  72.9 0.0 copy-start.3
  72.9 0.0 collective-permute-done.5
  72.9 1.5 %collective-permute-done.4 = f32[3,2,1,128]{3,2,1,0:T(1,128)S(1)} collective-permute-done((f32[3,2,1,128]{3,2,1,0:T(1,128)S(1)}, f32[3,2,1,128]{3,2,1,0:T(1,128)S(1)}, u32[]{:S(2)}, u32[]{:S(2)}) %collective-permute-start.4) | collective-permute-done | bytes 3104 | tf_op jit(solution)/shard_map/ppermute | solution.py:266
  74.4 0.0 copy-done.3
  74.4 0.1 fusion
  74.5 0.0 slice-start
  74.6 1.9 %collective-permute-start.6 = (f32[3,24,128]{2,1,0:T(8,128)S(1)}, f32[3,24,128]{2,1,0:T(8,128)S(1)}, u32[]{:S(2)}, u32[]{:S(2)}) collective-permute-start(f32[3,24,128]{2,1,0:T(8,128)S(1)} %get-tuple-element.20), channel_id=1, source_target_pairs={{0,4},{4,0},{8,12},{12,8},{16,20},{20,16},{24,28},{28,24},{32,36},... | collective-permute-start | bytes 110600 | tf_op jit(solution)/shard_map/ppermute | solution.py:259
  76.5 0.0 slice-done
  76.5 0.0 slice-start.1
  76.5 0.7 copy.34.own
  77.2 0.0 slice-start.2
  77.2 9.6 %collective-permute-start.7 = (f32[3,24,128]{2,1,0:T(8,128)S(1)}, f32[3,24,128]{2,1,0:T(8,128)S(1)}, u32[]{:S(2)}, u32[]{:S(2)}) collective-permute-start(f32[3,24,128]{2,1,0:T(8,128)S(1)} %get-tuple-element.19), channel_id=1, source_target_pairs={{4,8},{8,4},{12,16},{16,12},{20,24},{24,20},{28,32},{32,28},{36,40... | collective-permute-start | bytes 110600 | tf_op jit(solution)/shard_map/ppermute | solution.py:259
  86.8 0.0 collective-permute-done.6
  86.8 0.0 slice-done.1
  86.8 0.6 pad_maximum_fusion.2.near
  87.4 3.3 %collective-permute-done.7 = f32[3,24,128]{2,1,0:T(8,128)S(1)} collective-permute-done((f32[3,24,128]{2,1,0:T(8,128)S(1)}, f32[3,24,128]{2,1,0:T(8,128)S(1)}, u32[]{:S(2)}, u32[]{:S(2)}) %collective-permute-start.7) | collective-permute-done | bytes 36896 | tf_op jit(solution)/shard_map/ppermute | solution.py:259
  90.7 0.0 slice-done.2
  90.7 0.6 pad_maximum_fusion.3.far
  91.4 31.1 %forces1.1 = (f32[3,2,24,128]{3,2,1,0:T(8,128)}, f32[3,2,24,128]{3,2,1,0:T(8,128)}, f32[3,2,24,128]{3,2,1,0:T(8,128)}) custom-call(s32[1]{0:T(128)} %bitcast.parity, f32[6,2,24,128]{3,2,1,0:T(8,128)} %copy.34.own, f32[6,24,128]{2,1,0:T(8,128)} %pad_maximum_fusion.2.near, f32[6,24,128]{2,1,0:T(8,128)} %pad_maximum_fusion.3.far, ...), custom_call_target="tpu_custom_call" | custom-call | tf_op jit(solution)/shard_map/forces1/pallas_call | solution.py:231
  122.4 0.0 copy-start.8
  122.4 1.5 %slice.59 = f32[3,2,16,128]{3,2,1,0:T(8,128)} slice(f32[3,2,24,128]{3,2,1,0:T(8,128)} %get-tuple-element.10), slice={[0:3], [0:2], [2:18], [0:128]} | slice | bytes 98304 | tf_op jit(solution)/shard_map/slice | solution.py:302
  124.0 0.0 copy-start.7
  124.0 0.0 copy-done.8
  124.0 0.6 slice.60
  124.6 0.3 copy-done.7
  124.9 0.6 slice.61
  (15 shorter events, 0.1 us)
Async XLA Ops:
  0.6 0.9 copy-start.9
  0.6 0.9 copy-start.11
  0.7 1.0 copy-start.10
  1.5 0.8 copy-start.6
  1.6 0.8 copy-start.4
  1.6 0.8 copy-start.5
  2.4 12.5 %collective-permute-start.1 = (f32[6,2,1,128]{3,2,0,1:T(1,128)S(1)}, f32[6,2,1,128]{3,2,0,1:T(1,128)S(1)}, u32[]{:S(2)}, u32[]{:S(2)}) collective-permute-start(f32[6,2,1,128]{3,2,0,1:T(1,128)S(1)} %get-tuple-element.18), channel_id=1, source_target_pairs={{1,0},{2,1},{3,2},{5,4},{6,5},{7,6},{9,8},{10,9},{11,10},{13,12},{... | collective-permute-start | bytes 18440 | tf_op jit(solution)/shard_map/ppermute | solution.py:267
  13.0 5.5 %collective-permute-start = (f32[6,2,1,128]{3,2,0,1:T(1,128)S(1)}, f32[6,2,1,128]{3,2,0,1:T(1,128)S(1)}, u32[]{:S(2)}, u32[]{:S(2)}) collective-permute-start(f32[6,2,1,128]{3,2,0,1:T(1,128)S(1)} %get-tuple-element.17), channel_id=1, source_target_pairs={{0,1},{1,2},{2,3},{4,5},{5,6},{6,7},{8,9},{9,10},{10,11},{12,13},{... | collective-permute-start | bytes 18440 | tf_op jit(solution)/shard_map/ppermute | solution.py:266
  18.6 54.3 %copy-start = (f32[6,2,24,128]{3,2,0,1:T(8,128)}, f32[6,2,24,128]{3,2,0,1:T(8,128)S(1)}, u32[]{:S(2)}) copy-start(f32[6,2,24,128]{3,2,0,1:T(8,128)S(1)} %select_select_fusion) | copy-start | bytes 442372
  18.7 14.0 %collective-permute-start.2 = (f32[6,24,128]{2,1,0:T(8,128)S(1)}, f32[6,24,128]{2,1,0:T(8,128)S(1)}, u32[]{:S(2)}, u32[]{:S(2)}) collective-permute-start(f32[6,24,128]{2,1,0:T(8,128)S(1)} %get-tuple-element.16), channel_id=1, source_target_pairs={{0,4},{4,0},{8,12},{12,8},{16,20},{20,16},{24,28},{28,24},{32,36},... | collective-permute-start | bytes 221192 | tf_op jit(solution)/shard_map/ppermute | solution.py:259
  20.6 14.0 %collective-permute-start.3 = (f32[6,24,128]{2,1,0:T(8,128)S(1)}, f32[6,24,128]{2,1,0:T(8,128)S(1)}, u32[]{:S(2)}, u32[]{:S(2)}) collective-permute-start(f32[6,24,128]{2,1,0:T(8,128)S(1)} %get-tuple-element.15), channel_id=1, source_target_pairs={{4,8},{8,4},{12,16},{16,12},{20,24},{24,20},{28,32},{32,28},{36,40... | collective-permute-start | bytes 221192 | tf_op jit(solution)/shard_map/ppermute | solution.py:259
  32.7 1.9 %copy-start.1 = (f32[6,24,128]{2,1,0:T(8,128)}, f32[6,24,128]{2,1,0:T(8,128)S(1)}, u32[]{:S(2)}) copy-start(f32[6,24,128]{2,1,0:T(8,128)S(1)} %collective-permute-done.2.near) | copy-start | bytes 221188
  34.6 0.6 copy-start.2
  67.0 5.9 %collective-permute-start.5 = (f32[3,2,1,128]{3,2,1,0:T(1,128)S(1)}, f32[3,2,1,128]{3,2,1,0:T(1,128)S(1)}, u32[]{:S(2)}, u32[]{:S(2)}) collective-permute-start(f32[3,2,1,128]{3,2,1,0:T(1,128)S(1)} %get-tuple-element.22), channel_id=1, source_target_pairs={{1,0},{2,1},{3,2},{5,4},{6,5},{7,6},{9,8},{10,9},{11,10},{13,12},{... | collective-permute-start | bytes 9224 | tf_op jit(solution)/shard_map/ppermute | solution.py:267
  69.0 5.5 %collective-permute-start.4 = (f32[3,2,1,128]{3,2,1,0:T(1,128)S(1)}, f32[3,2,1,128]{3,2,1,0:T(1,128)S(1)}, u32[]{:S(2)}, u32[]{:S(2)}) collective-permute-start(f32[3,2,1,128]{3,2,1,0:T(1,128)S(1)} %get-tuple-element.21), channel_id=1, source_target_pairs={{0,1},{1,2},{2,3},{4,5},{5,6},{6,7},{8,9},{9,10},{10,11},{12,13},{... | collective-permute-start | bytes 9224 | tf_op jit(solution)/shard_map/ppermute | solution.py:266
  72.9 1.6 %copy-start.3 = (f32[3,2,24,128]{3,2,1,0:T(8,128)S(1)}, f32[3,2,24,128]{3,2,1,0:T(8,128)}, u32[]{:S(2)}) copy-start(f32[3,2,24,128]{3,2,1,0:T(8,128)} %get-tuple-element.8) | copy-start | bytes 221188
  74.5 2.0 %slice-start = ((f32[6,2,24,128]{3,2,0,1:T(8,128)}), f32[3,2,24,128]{3,2,0,1:T(8,128)S(1)}, s32[]{:S(2)}) async-start(f32[6,2,24,128]{3,2,0,1:T(8,128)} %copy-done), calls=%async_computation | async-start | bytes 147456 | tf_op jit(solution)/shard_map/slice | solution.py:298
  74.6 12.2 %collective-permute-start.6 = (f32[3,24,128]{2,1,0:T(8,128)S(1)}, f32[3,24,128]{2,1,0:T(8,128)S(1)}, u32[]{:S(2)}, u32[]{:S(2)}) collective-permute-start(f32[3,24,128]{2,1,0:T(8,128)S(1)} %get-tuple-element.20), channel_id=1, source_target_pairs={{0,4},{4,0},{8,12},{12,8},{16,20},{20,16},{24,28},{28,24},{32,36},... | collective-permute-start | bytes 110600 | tf_op jit(solution)/shard_map/ppermute | solution.py:259
  76.5 10.3 %slice-start.1 = ((f32[6,24,128]{2,1,0:T(8,128)}), f32[3,24,128]{2,1,0:T(8,128)S(1)}, s32[]{:S(2)}) async-start(f32[6,24,128]{2,1,0:T(8,128)} %copy-done.1), calls=%async_computation.1 | async-start | bytes 73728 | tf_op jit(solution)/shard_map/slice | solution.py:299
  77.2 13.5 %slice-start.2 = ((f32[6,24,128]{2,1,0:T(8,128)}), f32[3,24,128]{2,1,0:T(8,128)S(1)}, s32[]{:S(2)}) async-start(f32[6,24,128]{2,1,0:T(8,128)} %copy-done.2), calls=%async_computation.2 | async-start | bytes 73728 | tf_op jit(solution)/shard_map/slice | solution.py:300
  77.2 13.5 %collective-permute-start.7 = (f32[3,24,128]{2,1,0:T(8,128)S(1)}, f32[3,24,128]{2,1,0:T(8,128)S(1)}, u32[]{:S(2)}, u32[]{:S(2)}) collective-permute-start(f32[3,24,128]{2,1,0:T(8,128)S(1)} %get-tuple-element.19), channel_id=1, source_target_pairs={{4,8},{8,4},{12,16},{16,12},{20,24},{24,20},{28,32},{32,28},{36,40... | collective-permute-start | bytes 110600 | tf_op jit(solution)/shard_map/ppermute | solution.py:259
  122.4 1.5 %copy-start.8 = (f32[3,2,24,128]{3,2,1,0:T(8,128)S(1)}, f32[3,2,24,128]{3,2,1,0:T(8,128)}, u32[]{:S(2)}) copy-start(f32[3,2,24,128]{3,2,1,0:T(8,128)} %get-tuple-element.11) | copy-start | bytes 221188
  124.0 0.9 copy-start.7

commit v2 on v1

v2 whole, which is shorter than its diff:
```python
import functools

import jax
import jax.numpy as jnp
from jax import lax
from jax.experimental import pallas as pl
from jax.experimental.pallas import tpu as pltpu
from jax.sharding import PartitionSpec as P

DT = 0.05
CORE = 0.09
CHANNELS = 6
DEPTH = 16
ROWS = 24
USED = DEPTH + 2
RAW_A, RAW_W, RAW_Q, RAW_B = 0, 32, 48, 56
RAW = 120
BINS = 2 * ROWS
BF = jnp.bfloat16
F32 = jnp.float32


def split3(value):
    high = value.astype(BF).astype(F32)
    rest = value - high
    mid = rest.astype(BF).astype(F32)
    return high, mid, rest - mid


def raw_features(raw, group, fields, targets):
    x, y, z, charge, names = fields
    zero = jnp.zeros((8, 128), F32)
    one = jnp.ones((8, 128), F32)

    def put(base, value):
        raw[pl.ds(group * 8 * RAW + base, 8, stride=RAW), :] = value

    for k, coord in enumerate((x, y, z)):
        h, m, l = split3(coord)
        base = RAW_A + (0, 6, 22)[k]
        for i, value in enumerate((h, h, m, h, l, m)):
            put(base + i, 2 * value)
        if targets and k < 2:
            for i, value in enumerate((h, m, h, l, h, m)):
                put(RAW_B + 6 * k + i, value)
        for i, value in enumerate((h, m, l)):
            put(RAW_W + 4 * i + k, value)
    flat = x * x + y * y
    for i, value in enumerate(split3(-(flat + z * z))):
        put(RAW_A + 16 + i, one)
        put(RAW_A + 19 + i, value)
    put(RAW_W + 3, one)
    put(RAW_W + 7, zero)
    put(RAW_W + 11, zero)
    for i in range(12, 16):
        put(RAW_A + i, zero)
        put(RAW_A + 16 + i, zero)
        put(RAW_W + i, zero)
    for i, value in enumerate(split3(charge)):
        put(RAW_Q + i, value)
    put(RAW_Q + 3, names)
    for i in range(4, 8):
        put(RAW_Q + i, zero)
    if not targets:
        return
    for v, shift in enumerate((-1.0, 0.0, 1.0)):
        other = z + shift
        base = RAW_B + 16 + 16 * v
        for i, value in enumerate(split3((1.0 - flat) - other * other)):
            put(base + i, value)
            put(base + 3 + i, one)
        h, m, l = split3(other)
        for i, value in enumerate((h, m, h, l, h, m)):
            put(base + 6 + i, value)
        for i in range(12, 16):
            put(base + i, zero)
            if v == 0:
                put(RAW_B + i, zero)


def pack_features(raw, code, repulsion, at_ref, w_ref, qi_ref, b_ref):
    code_rows = lax.broadcasted_iota(jnp.int32, (16, 128), 0).astype(F32) + 1.0
    row16 = lax.broadcasted_iota(jnp.int32, (16, 128), 0)
    spread = jnp.where(row16 < 3, 1.0, 0.0).astype(BF)
    table = 0.5 * (repulsion[...] + repulsion[...].T)
    table = jnp.concatenate(split3(table), axis=0).astype(BF)
    half_tile = jnp.zeros((8, 128), F32)

    def one_bin(n, carry):
        b = (n // USED) * ROWS + n % USED
        base = pl.multiple_of(b * RAW, 8)
        hot = (code[pl.ds(b, 1), :] == code_rows).astype(F32).astype(BF)
        lookup = jnp.dot(table, hot, preferred_element_type=F32).astype(BF)
        tail = jnp.concatenate([raw[pl.ds(base + RAW_Q, 8), :], half_tile], 0).astype(BF)
        rows = jnp.concatenate([raw[pl.ds(base + RAW_A, 32), :].astype(BF), lookup, tail], 0)
        at_ref[b] = rows.T
        w_ref[b] = raw[pl.ds(base + RAW_W, 16), :].astype(BF)
        qi_ref[b] = lax.dot_general(tail, spread, (((0,), (0,)), ((), ())), preferred_element_type=F32)
        if b_ref is not None:
            b_ref[b, 0:64, :] = raw[pl.ds(base + RAW_B, 64), :].astype(BF)
            b_ref[b, 64:80, :] = hot
        return carry

    lax.fori_loop(0, 2 * USED, one_bin, 0, unroll=6)


def place_of(row):
    return jnp.where(row < 0, DEPTH, jnp.where(row >= DEPTH, DEPTH + 1, row))


def tilts():
    row16 = lax.broadcasted_iota(jnp.int32, (16, 128), 0)
    return {dz: jnp.where(row16 == 12, float(-dz), 0.0).astype(BF) for dz in (-1, 1)}


def scalar_block(reach, soft, charges):
    inside = jnp.maximum(reach, 0.0)
    inverse = lax.rsqrt((1.0 + CORE) - reach)
    coulomb = charges * inside * (inverse * inverse * inverse)
    scalar = (soft + coulomb) * inside
    high = scalar.astype(BF)
    return high, (scalar - high.astype(F32)).astype(BF)


def pipelined(product, scalar, reduce, buffers):
    for ref in buffers:
        ref[...] = jnp.zeros_like(ref)

    def body(n, carry):
        for half in (0, 1):
            step = 2 * n + half
            reduce(jnp.maximum(step - 2, 0), half)
            product(jnp.minimum(step, DEPTH - 1), half)
            scalar(jnp.clip(step - 1, 0, DEPTH - 1), 1 - half)
        return carry

    lax.fori_loop(0, DEPTH // 2 + 1, body, 0)


def inner_kernel(own, repulsion, acc, b_ref, raw, at_ref, w_ref, qi_ref, ut, sh):
    for group in range(6):
        col, inner = divmod(group, 3)
        at = slice(inner * 8, inner * 8 + 8)
        fields = [own[c, col, at, :] for c in (0, 1, 2, 3, 5)]
        fields[0] = fields[0] + (col - 0.5)
        raw_features(raw, group, fields, inner < 2)
    code = own.at[4].reshape(BINS, 128)
    charge = own.at[3].reshape(BINS, 128)
    pack_features(raw, code, repulsion, at_ref, w_ref, qi_ref, b_ref)
    tilt = tilts()
    row16 = lax.broadcasted_iota(jnp.int32, (16, 128), 0)
    spread_names = jnp.where(row16 == 3, 1.0, 0.0).astype(BF)
    slot = lax.broadcasted_iota(jnp.int32, (16, 128), 1).astype(F32)
    pairs = [(col, dz) for dz in (-1, 0, 1) for col in (0, 1)]

    def source(row, col, dz):
        return col * ROWS + place_of(row - dz)

    def product(row, slot_id):
        for k, (col, dz) in enumerate(pairs):
            b = source(row, col, dz)
            lhs = at_ref[b]
            sides = [
                jnp.concatenate(
                    [b_ref[t * ROWS + row, 0:16, :], b_ref[t * ROWS + row, 32 + 16 * dz : 48 + 16 * dz, :]], 0
                )
                for t in (0, 1)
            ]
            reach = jnp.dot(lhs[:, 0:32], jnp.concatenate(sides, 1), preferred_element_type=F32)
            hots = jnp.concatenate([b_ref[t * ROWS + row, 64:80, :] for t in (0, 1)], 1)
            soft = jnp.dot(lhs[:, 32:80], jnp.concatenate([hots] * 3, 0), preferred_element_type=F32)
            if dz == 0:
                listed = lax.dot_general(
                    own_names(b), spread_names, (((0,), (0,)), ((), ())), preferred_element_type=F32
                )
                first = (listed[0:16, :] == slot).astype(F32)
                second = (listed[16:32, :] == slot).astype(F32)
                hits = lax.dot_general(
                    jnp.concatenate([first, second], 0).astype(BF),
                    jnp.concatenate([second, first], 0).astype(BF),
                    (((0,), (0,)), ((), ())),
                    preferred_element_type=F32,
                )
                here = slice(128 * col, 128 * col + 128)
                there = slice(128 * (1 - col), 128 * (1 - col) + 128)
                ut[slot_id, k, :, here] = jnp.where(hits > 0.0, -1.0, reach[:, here])
                ut[slot_id, k, :, there] = reach[:, there]
            else:
                ut[slot_id, k, :, 0:256] = reach
            ut[slot_id, k, :, 256:512] = soft

    def own_names(b):
        base = pl.multiple_of(b * RAW, 8)
        tail = raw[pl.ds(base + RAW_Q, 8), :]
        return jnp.concatenate([tail, jnp.zeros((8, 128), F32)], 0).astype(BF)

    def scalar(row, slot_id):
        others = [charge[pl.ds(t * ROWS + row, 1), :] for t in (0, 1)]
        for k, (col, dz) in enumerate(pairs):
            b = source(row, col, dz)
            for i in range(0, 128, 16):
                mine = qi_ref[b, i : i + 16, :]
                for t in (0, 1):
                    lanes = slice(128 * t, 128 * t + 128)
                    high, low = scalar_block(
                        ut[slot_id, k, i : i + 16, lanes],
                        ut[slot_id, k, i : i + 16, 256 + 128 * t : 384 + 128 * t],
                        mine * others[t],
                    )
                    sh[slot_id, 0, 128 * k + i : 128 * k + i + 16, lanes] = high
                    sh[slot_id, 1, 128 * k + i : 128 * k + i + 16, lanes] = low

    def reduce(row, slot_id):
        parts = []
        for col, dz in pairs:
            w = w_ref[source(row, col, dz)]
            parts.append(w + tilt[dz] if dz else w)
        w = jnp.concatenate(parts, 1)
        total = jnp.dot(w, sh[slot_id, 0], preferred_element_type=F32)
        total = total + jnp.dot(w, sh[slot_id, 1], preferred_element_type=F32)
        acc[row] = total[:, :128]
        acc[DEPTH + row] = total[:, 128:]

    pipelined(product, scalar, reduce, (ut, sh))


def outer_kernel(
    step, parity, own, near, far, acc_in, b_ref, vel, repulsion, pos_out, vel_out, frc_out,
    raw, at_ref, w_ref, qi_ref, ut, sh, acc, code,
):
    swap = parity[0] == 1
    for group in range(6):
        side, inner = divmod(group, 3)
        at = slice(inner * 8, inner * 8 + 8)
        first, second = (far, near) if side == 0 else (near, far)
        fields = [jnp.where(swap, second[c, at, :], first[c, at, :]) for c in (0, 1, 2, 3, 4)]
        code[group * 8 : group * 8 + 8, :] = fields.pop()
        fields[0] = fields[0] + (-1.5, 1.5)[side]
        raw_features(raw, group, fields + [jnp.zeros((8, 128), F32)], False)
    pack_features(raw, code, repulsion, at_ref, w_ref, qi_ref, None)
    charge = own.at[3].reshape(BINS, 128)
    tilt = tilts()
    pairs = [(col, dz) for col in (0, 1) for dz in (-1, 0, 1)]
    zero_d = jnp.zeros((32, 128), BF)
    zero_t = jnp.zeros((48, 128), BF)

    def source(row, col, dz):
        return col * ROWS + place_of(row - dz)

    def product(row, slot_id):
        for k, (col, dz) in enumerate(pairs):
            lhs = at_ref[source(row, col, dz)][:, 0:80]
            target = col * ROWS + row
            hot = b_ref[target, 64:80, :]
            left = jnp.concatenate(
                [b_ref[target, 0:16, :], b_ref[target, 32 + 16 * dz : 48 + 16 * dz, :], zero_t], 0
            )
            right = jnp.concatenate([zero_d, hot, hot, hot], 0)
            ut[slot_id, k] = jnp.dot(lhs, jnp.concatenate([left, right], 1), preferred_element_type=F32)

    def scalar(row, slot_id):
        others = [charge[pl.ds(t * ROWS + row, 1), :] for t in (0, 1)]
        for k, (col, dz) in enumerate(pairs):
            b = source(row, col, dz)
            for i in range(0, 128, 16):
                high, low = scalar_block(
                    ut[slot_id, k, i : i + 16, 0:128],
                    ut[slot_id, k, i : i + 16, 128:256],
                    qi_ref[b, i : i + 16, :] * others[col],
                )
                at = 128 * (k % 3) + i
                sh[slot_id, col, at : at + 16, :] = high
                sh[slot_id, col, 384 + at : 400 + at, :] = low

    def reduce(row, slot_id):
        for side in (0, 1):
            parts = []
            for col, dz in pairs:
                if col == side:
                    w = w_ref[source(row, col, dz)]
                    parts.append(w + tilt[dz] if dz else w)
            w = jnp.concatenate(parts + parts, 1)
            acc[side * DEPTH + row] = acc_in[side * DEPTH + row] + jnp.dot(
                w, sh[slot_id, side], preferred_element_type=F32
            )

    pipelined(product, scalar, reduce, (ut, sh))

    flat = acc.reshape(2 * DEPTH * 16, 128)
    for group in range(4):
        col, inner = divmod(group, 2)
        at = slice(inner * 8, inner * 8 + 8)

        def take(k):
            return flat[pl.ds(group * 128 + k, 8, stride=16), :]

        count = take(3)
        for c in range(3):
            here = own[c, col, at, :]
            back = (take(c) + take(4 + c)) + take(8 + c)
            if c == 2:
                back = back + take(12)
            frame = here + (col - 0.5) if c == 0 else here
            force = frame * count - back
            v = vel[c, col, at, :] + 0.5 * DT * force
            if step == 0:
                v = v + 0.5 * DT * force
                here = here + DT * v
            pos_out[c, col, at, :] = here
            vel_out[c, col, at, :] = v
            frc_out[c, col, at, :] = force


VMEM = pl.BlockSpec(memory_space=pltpu.VMEM)
FEATURES = [
    pltpu.VMEM((BINS * RAW, 128), F32),
    pltpu.VMEM((BINS, 128, 96), BF),
    pltpu.VMEM((BINS, 16, 128), BF),
    pltpu.VMEM((BINS, 128, 128), F32),
]
LIMIT = pltpu.CompilerParams(vmem_limit_bytes=40 * 1024 * 1024)


def inner_call(step, own, repulsion):
    return pl.pallas_call(
        inner_kernel,
        out_shape=(
            jax.ShapeDtypeStruct((2 * DEPTH, 16, 128), F32),
            jax.ShapeDtypeStruct((BINS, 80, 128), BF),
        ),
        in_specs=[VMEM, VMEM],
        out_specs=(VMEM, VMEM),
        scratch_shapes=FEATURES
        + [pltpu.VMEM((2, 6, 128, 512), F32), pltpu.VMEM((2, 2, 768, 256), BF)],
        compiler_params=LIMIT,
        name=f"inner{step}",
    )(own, repulsion)


def outer_call(step, parity, own, near, far, acc, features, vel, repulsion):
    out = jax.ShapeDtypeStruct((3, 2, DEPTH, 128), F32)
    return pl.pallas_call(
        functools.partial(outer_kernel, step),
        out_shape=(out, out, out),
        in_specs=[pl.BlockSpec(memory_space=pltpu.SMEM)] + [VMEM] * 7,
        out_specs=(VMEM, VMEM, VMEM),
        scratch_shapes=FEATURES
        + [
            pltpu.VMEM((2, 6, 128, 256), F32),
            pltpu.VMEM((2, 2, 768, 128), BF),
            pltpu.VMEM((2 * DEPTH, 16, 128), F32),
            pltpu.VMEM((BINS, 128), F32),
        ],
        compiler_params=LIMIT,
        name=f"outer{step}",
    )(parity, own, near, far, acc, features, vel, repulsion)


def swap_pairs(value, odd):
    count = lax.axis_size("gx")
    start = 1 if odd else 0
    route = []
    for i in range(start, count + start, 2):
        a, b = i % count, (i + 1) % count
        route += [(a, b), (b, a)]
    return lax.ppermute(value, "gx", route)


def with_rows(block):
    count = lax.axis_size("gz")
    up = [(i, i + 1) for i in range(count - 1)]
    down = [(b, a) for a, b in up]
    low = lax.ppermute(block[:, :, DEPTH - 1 :], "gz", up)
    high = lax.ppermute(block[:, :, :1], "gz", down)
    pad = jnp.zeros(block.shape[:2] + (ROWS - USED, block.shape[3]), F32)
    return jnp.concatenate([block, low, high, pad], 2)


def exchanged(block, parity):
    own = with_rows(block)
    far = swap_pairs(jnp.where(parity == 1, own[:, 1], own[:, 0]), True)
    near = swap_pairs(jnp.where(parity == 1, own[:, 0], own[:, 1]), False)
    return own, near, far


def local(positions, velocities, forces, charge, atom_type, bin_count, exclusions, repulsion):
    columns, depth, slots = positions.shape[1:]
    velocities = velocities + 0.5 * DT * forces
    positions = positions + DT * velocities
    slot_ids = jnp.arange(slots, dtype=jnp.int32)
    live = slot_ids < bin_count[..., None]
    code = jnp.where(live, atom_type + 1, 0).astype(F32)
    live_charge = jnp.where(live, charge, 0.0)
    names = exclusions.reshape(columns, depth, -1).astype(F32)
    names = jnp.pad(names, ((0, 0), (0, 0), (0, slots - names.shape[-1])))
    packed = jnp.concatenate([positions, live_charge[None], code[None], names[None]], axis=0)
    parity = lax.axis_index("gx") % 2
    flag = parity.astype(jnp.int32).reshape(1)
    own, near, far = exchanged(packed, parity)
    acc, features = inner_call(0, own, repulsion)
    p, v, _ = outer_call(0, flag, own, near, far, acc, features, velocities, repulsion)
    p, near_p, far_p = exchanged(p, parity)
    own = jnp.concatenate([p, own[3:]], 0)
    near = jnp.concatenate([near_p, near[3:]], 0)
    far = jnp.concatenate([far_p, far[3:]], 0)
    acc, features = inner_call(1, own, repulsion)
    return outer_call(1, flag, own, near, far, acc, features, v, repulsion)


def solution(mesh):
    grid = P(None, "gx", "gz", None)
    return jax.shard_map(
        local,
        mesh=mesh,
        in_specs=(
            grid, grid, grid,
            P("gx", "gz", None), P("gx", "gz", None), P("gx", "gz"), P("gx", "gz", None, None), P(),
        ),
        out_specs=(grid, grid, grid),
        check_vma=False,
    )
```

time: 126 us -> 95.2 us (0.76)
  the two profiles are of different devices: /device:TPU:64 before, /device:TPU:1 now
where the time goes in v2:
time: 95.2 us; the launch traced here: 94.6 us
  Pallas kernels  48.7 us (51%)
  starting transfers between devices  40.1 us (42%)
  local copies, waits for them, and re-layouts  2.3 us (2%)
  waiting for transfers between devices  1.35 us (1%)
  other arithmetic  1.12 us (1%)
  between operations  0.98 us (1%)
    pallas_call x2, Pallas kernels, inner_call(): pl.pallas_call(inner_kernel, out_shape=(jax.ShapeDtypeStruct((2 * DEPTH,...  32.6 us
    ppermute x4, starting transfers between devices, swap_pairs(): return lax.ppermute(value, 'gx', route)  27.5 us
    pallas_call x2, Pallas kernels, outer_call(): pl.pallas_call(functools.partial(outer_kernel, step), out_shape=(out, out...  16.1 us
    ppermute x2, starting transfers between devices, with_rows(): low = lax.ppermute(block[:, :, DEPTH - 1:], 'gz', up)  9.97 us
    ppermute x2, starting transfers between devices, with_rows(): high = lax.ppermute(block[:, :, :1], 'gz', down)  2.57 us
  transfers between devices with their start and end apart: 8, of which 2 were waited for; matrix products, arithmetic and copies ran while one was open for 0% of the time, Pallas kernels for 34%

profile of v2, /device:TPU:1, one launch (start us, length us, event | category | flops | bytes accessed | tf_op | source)
XLA Modules:
  0.0 94.6 jit_solution(11598941939215016290)
XLA Ops:
  0.6 0.0 copy-start.7
  0.6 0.0 copy-start.9
  0.7 0.0 copy-start.8
  0.7 0.8 convert_element_type.12
  1.5 0.0 copy-start.6
  1.5 0.1 convert_element_type.13
  1.6 0.0 copy-done.7
  1.6 0.0 copy-done.9
  1.6 0.0 copy-start.4
  1.6 0.0 copy-start.5
  1.6 0.1 convert_bitcast_fusion
  1.6 0.0 copy-done.8
  1.6 0.1 pad_bitcast_fusion
  1.7 0.5 copy-done.6
  2.3 0.1 copy-done.4
  2.4 0.0 copy-done.5
  2.4 1.3 %collective-permute-start.1 = (f32[6,2,1,128]{3,2,0,1:T(1,128)S(1)}, f32[6,2,1,128]{3,2,0,1:T(1,128)S(1)}, u32[]{:S(2)}, u32[]{:S(2)}) collective-permute-start(f32[6,2,1,128]{3,2,0,1:T(1,128)S(1)} %get-tuple-element.20), channel_id=1, source_target_pairs={{1,0},{2,1},{3,2},{5,4},{6,5},{7,6},{9,8},{10,9},{11,10},{13,12},{... | collective-permute-start | bytes 18440 | tf_op jit(solution)/shard_map/ppermute | solution.py:374
  3.7 5.4 %collective-permute-start = (f32[6,2,1,128]{3,2,0,1:T(1,128)S(1)}, f32[6,2,1,128]{3,2,0,1:T(1,128)S(1)}, u32[]{:S(2)}, u32[]{:S(2)}) collective-permute-start(f32[6,2,1,128]{3,2,0,1:T(1,128)S(1)} %get-tuple-element.19), channel_id=1, source_target_pairs={{0,1},{1,2},{2,3},{4,5},{5,6},{6,7},{8,9},{9,10},{10,11},{12,13},{... | collective-permute-start | bytes 18440 | tf_op jit(solution)/shard_map/ppermute | solution.py:373
  9.2 0.1 pad.24.clone
  9.3 0.0 collective-permute-done.1
  9.3 0.6 collective-permute-done
  9.9 0.1 maximum_maximum_fusion
  10.0 0.0 copy-start.3
  10.0 12.1 %collective-permute-start.2 = (f32[6,24,128]{2,1,0:T(8,128)S(1)}, f32[6,24,128]{2,1,0:T(8,128)S(1)}, u32[]{:S(2)}, u32[]{:S(2)}) collective-permute-start(f32[6,24,128]{2,1,0:T(8,128)S(1)} %get-tuple-element.18), channel_id=1, source_target_pairs={{0,4},{4,0},{8,12},{12,8},{16,20},{20,16},{24,28},{28,24},{32,36},... | collective-permute-start | bytes 221192 | tf_op jit(solution)/shard_map/ppermute | solution.py:366
  22.1 1.9 %collective-permute-start.3 = (f32[6,24,128]{2,1,0:T(8,128)S(1)}, f32[6,24,128]{2,1,0:T(8,128)S(1)}, u32[]{:S(2)}, u32[]{:S(2)}) collective-permute-start(f32[6,24,128]{2,1,0:T(8,128)S(1)} %get-tuple-element.17), channel_id=1, source_target_pairs={{4,8},{8,4},{12,16},{16,12},{20,24},{24,20},{28,32},{32,28},{36,40... | collective-permute-start | bytes 221192 | tf_op jit(solution)/shard_map/ppermute | solution.py:366
  24.1 0.0 copy-start.2
  24.1 0.7 copy-done.2
  24.8 16.3 %inner0.1 = (f32[32,16,128]{2,1,0:T(8,128)S(1)}, bf16[48,80,128]{2,1,0:T(8,128)(2,1)S(1)}) custom-call(f32[6,2,24,128]{3,2,1,0:T(8,128)S(1)} %copy.16.own, f32[16,16]{1,0:T(8,128)S(1)} %copy-done.2), custom_call_target="tpu_custom_call" | custom-call | tf_op jit(solution)/shard_map/inner0/pallas_call | solution.py:325
  41.1 0.0 collective-permute-done.2.near
  41.1 0.0 copy-start
  41.1 0.0 collective-permute-done.3.far
  41.1 0.0 copy-start.1
  41.1 8.1 %outer0.1 = (f32[3,2,16,128]{3,2,1,0:T(8,128)S(1)}, f32[3,2,16,128]{3,2,1,0:T(8,128)S(1)}, f32[3,2,16,128]{3,2,1,0:T(8,128)}) custom-call(s32[1]{0:T(128)} %bitcast.parity, f32[6,2,24,128]{3,2,1,0:T(8,128)S(1)} %copy.16.own, f32[6,24,128]{2,1,0:T(8,128)S(1)} %collective-permute-done.2.near, f32[6,24,128]{2,1,0:T(8,128)S(1)} %collective-permute-done.3.far, ...), custom_call_target="tpu_custom_call" | custom-call | tf_op jit(solution)/shard_map/outer0/pallas_call | solution.py:342
  49.2 1.3 %collective-permute-start.5 = (f32[3,2,1,128]{3,2,0,1:T(1,128)S(1)}, f32[3,2,1,128]{3,2,0,1:T(1,128)S(1)}, u32[]{:S(2)}, u32[]{:S(2)}) collective-permute-start(f32[3,2,1,128]{3,2,0,1:T(1,128)S(1)} %get-tuple-element.24), channel_id=1, source_target_pairs={{1,0},{2,1},{3,2},{5,4},{6,5},{7,6},{9,8},{10,9},{11,10},{13,12},{... | collective-permute-start | bytes 9224 | tf_op jit(solution)/shard_map/ppermute | solution.py:374
  50.5 4.5 %collective-permute-start.4 = (f32[3,2,1,128]{3,2,0,1:T(1,128)S(1)}, f32[3,2,1,128]{3,2,0,1:T(1,128)S(1)}, u32[]{:S(2)}, u32[]{:S(2)}) collective-permute-start(f32[3,2,1,128]{3,2,0,1:T(1,128)S(1)} %get-tuple-element.23), channel_id=1, source_target_pairs={{0,1},{1,2},{2,3},{4,5},{5,6},{6,7},{8,9},{9,10},{10,11},{12,13},{... | collective-permute-start | bytes 9224 | tf_op jit(solution)/shard_map/ppermute | solution.py:373
  55.0 0.0 copy-done.3
  55.0 0.0 copy-done
  55.0 0.0 copy-done.1
  55.0 0.0 collective-permute-done.5
  55.1 0.7 collective-permute-done.4
  55.8 0.0 slice-start.2
  55.8 11.6 %collective-permute-start.6 = (f32[3,24,128]{2,1,0:T(8,128)S(1)}, f32[3,24,128]{2,1,0:T(8,128)S(1)}, u32[]{:S(2)}, u32[]{:S(2)}) collective-permute-start(f32[3,24,128]{2,1,0:T(8,128)S(1)} %get-tuple-element.22), channel_id=1, source_target_pairs={{0,4},{4,0},{8,12},{12,8},{16,20},{20,16},{24,28},{28,24},{32,36},... | collective-permute-start | bytes 110600 | tf_op jit(solution)/shard_map/ppermute | solution.py:366
  67.4 0.0 slice-done.2
  67.5 0.0 slice-start
  67.5 1.9 %collective-permute-start.7 = (f32[3,24,128]{2,1,0:T(8,128)S(1)}, f32[3,24,128]{2,1,0:T(8,128)S(1)}, u32[]{:S(2)}, u32[]{:S(2)}) collective-permute-start(f32[3,24,128]{2,1,0:T(8,128)S(1)} %get-tuple-element.21), channel_id=1, source_target_pairs={{4,8},{8,4},{12,16},{16,12},{20,24},{24,20},{28,32},{32,28},{36,40... | collective-permute-start | bytes 110600 | tf_op jit(solution)/shard_map/ppermute | solution.py:366
  69.4 16.3 %inner1.1 = (f32[32,16,128]{2,1,0:T(8,128)S(1)}, bf16[48,80,128]{2,1,0:T(8,128)(2,1)S(1)}) custom-call(f32[6,2,24,128]{3,2,1,0:T(8,128)S(1)} %copy.22.own, f32[16,16]{1,0:T(8,128)S(1)} %copy-done.2), custom_call_target="tpu_custom_call" | custom-call | tf_op jit(solution)/shard_map/inner1/pallas_call | solution.py:325
  85.7 0.0 slice-start.1
  85.7 0.0 collective-permute-done.6
  85.7 0.0 slice-done
  85.8 0.0 collective-permute-done.7
  85.8 0.7 slice-done.1
  86.5 8.0 %outer1.1 = (f32[3,2,16,128]{3,2,1,0:T(8,128)}, f32[3,2,16,128]{3,2,1,0:T(8,128)}, f32[3,2,16,128]{3,2,1,0:T(8,128)}) custom-call(s32[1]{0:T(128)} %bitcast.parity, f32[6,2,24,128]{3,2,1,0:T(8,128)S(1)} %copy.22.own, f32[6,24,128]{2,1,0:T(8,128)S(1)} %pad_maximum_fusion.2.near, f32[6,24,128]{2,1,0:T(8,128)S(1)} %pad_maximum_fusion.3.far, ...), custom_call_target="tpu_custom_call" | custom-call | tf_op jit(solution)/shard_map/outer1/pallas_call | solution.py:342
  (14 shorter events, 0.1 us)
Async XLA Ops:
  0.6 0.9 copy-start.7
  0.6 0.9 copy-start.9
  0.7 1.0 %copy-start.8 = (f32[2,16,128]{2,1,0:T(8,128)S(1)}, f32[2,16,128]{2,1,0:T(8,128)}, u32[]{:S(2)}) copy-start(f32[2,16,128]{2,1,0:T(8,128)} %param.11) | copy-start | bytes 49156
  1.5 0.8 copy-start.6
  1.6 0.8 copy-start.4
  1.6 0.8 copy-start.5
  2.4 6.9 %collective-permute-start.1 = (f32[6,2,1,128]{3,2,0,1:T(1,128)S(1)}, f32[6,2,1,128]{3,2,0,1:T(1,128)S(1)}, u32[]{:S(2)}, u32[]{:S(2)}) collective-permute-start(f32[6,2,1,128]{3,2,0,1:T(1,128)S(1)} %get-tuple-element.20), channel_id=1, source_target_pairs={{1,0},{2,1},{3,2},{5,4},{6,5},{7,6},{9,8},{10,9},{11,10},{13,12},{... | collective-permute-start | bytes 18440 | tf_op jit(solution)/shard_map/ppermute | solution.py:374
  3.7 6.2 %collective-permute-start = (f32[6,2,1,128]{3,2,0,1:T(1,128)S(1)}, f32[6,2,1,128]{3,2,0,1:T(1,128)S(1)}, u32[]{:S(2)}, u32[]{:S(2)}) collective-permute-start(f32[6,2,1,128]{3,2,0,1:T(1,128)S(1)} %get-tuple-element.19), channel_id=1, source_target_pairs={{0,1},{1,2},{2,3},{4,5},{5,6},{6,7},{8,9},{9,10},{10,11},{12,13},{... | collective-permute-start | bytes 18440 | tf_op jit(solution)/shard_map/ppermute | solution.py:373
  10.0 45.0 %copy-start.3 = (f32[6,2,24,128]{3,2,0,1:T(8,128)}, f32[6,2,24,128]{3,2,0,1:T(8,128)S(1)}, u32[]{:S(2)}) copy-start(f32[6,2,24,128]{3,2,0,1:T(8,128)S(1)} %maximum_maximum_fusion) | copy-start | bytes 442372
  10.0 31.0 %collective-permute-start.2 = (f32[6,24,128]{2,1,0:T(8,128)S(1)}, f32[6,24,128]{2,1,0:T(8,128)S(1)}, u32[]{:S(2)}, u32[]{:S(2)}) collective-permute-start(f32[6,24,128]{2,1,0:T(8,128)S(1)} %get-tuple-element.18), channel_id=1, source_target_pairs={{0,4},{4,0},{8,12},{12,8},{16,20},{20,16},{24,28},{28,24},{32,36},... | collective-permute-start | bytes 221192 | tf_op jit(solution)/shard_map/ppermute | solution.py:366
  22.1 19.0 %collective-permute-start.3 = (f32[6,24,128]{2,1,0:T(8,128)S(1)}, f32[6,24,128]{2,1,0:T(8,128)S(1)}, u32[]{:S(2)}, u32[]{:S(2)}) collective-permute-start(f32[6,24,128]{2,1,0:T(8,128)S(1)} %get-tuple-element.17), channel_id=1, source_target_pairs={{4,8},{8,4},{12,16},{16,12},{20,24},{24,20},{28,32},{32,28},{36,40... | collective-permute-start | bytes 221192 | tf_op jit(solution)/shard_map/ppermute | solution.py:366
  24.1 0.7 copy-start.2
  41.1 13.9 %copy-start = (f32[6,24,128]{2,1,0:T(8,128)}, f32[6,24,128]{2,1,0:T(8,128)S(1)}, u32[]{:S(2)}) copy-start(f32[6,24,128]{2,1,0:T(8,128)S(1)} %collective-permute-done.2.near) | copy-start | bytes 221188
  41.1 13.9 %copy-start.1 = (f32[6,24,128]{2,1,0:T(8,128)}, f32[6,24,128]{2,1,0:T(8,128)S(1)}, u32[]{:S(2)}) copy-start(f32[6,24,128]{2,1,0:T(8,128)S(1)} %collective-permute-done.3.far) | copy-start | bytes 221188
  49.2 5.9 %collective-permute-start.5 = (f32[3,2,1,128]{3,2,0,1:T(1,128)S(1)}, f32[3,2,1,128]{3,2,0,1:T(1,128)S(1)}, u32[]{:S(2)}, u32[]{:S(2)}) collective-permute-start(f32[3,2,1,128]{3,2,0,1:T(1,128)S(1)} %get-tuple-element.24), channel_id=1, source_target_pairs={{1,0},{2,1},{3,2},{5,4},{6,5},{7,6},{9,8},{10,9},{11,10},{13,12},{... | collective-permute-start | bytes 9224 | tf_op jit(solution)/shard_map/ppermute | solution.py:374
  50.5 5.3 %collective-permute-start.4 = (f32[3,2,1,128]{3,2,0,1:T(1,128)S(1)}, f32[3,2,1,128]{3,2,0,1:T(1,128)S(1)}, u32[]{:S(2)}, u32[]{:S(2)}) collective-permute-start(f32[3,2,1,128]{3,2,0,1:T(1,128)S(1)} %get-tuple-element.23), channel_id=1, source_target_pairs={{0,1},{1,2},{2,3},{4,5},{5,6},{6,7},{8,9},{9,10},{10,11},{12,13},{... | collective-permute-start | bytes 9224 | tf_op jit(solution)/shard_map/ppermute | solution.py:373
  55.8 11.7 %slice-start.2 = ((f32[6,2,24,128]{3,2,0,1:T(8,128)}), f32[3,2,24,128]{3,2,0,1:T(8,128)S(1)}, s32[]{:S(2)}) async-start(f32[6,2,24,128]{3,2,0,1:T(8,128)} %copy-done.3), calls=%async_computation.2 | async-start | bytes 147456 | tf_op jit(solution)/shard_map/slice | solution.py:403
  55.8 29.9 %collective-permute-start.6 = (f32[3,24,128]{2,1,0:T(8,128)S(1)}, f32[3,24,128]{2,1,0:T(8,128)S(1)}, u32[]{:S(2)}, u32[]{:S(2)}) collective-permute-start(f32[3,24,128]{2,1,0:T(8,128)S(1)} %get-tuple-element.22), channel_id=1, source_target_pairs={{0,4},{4,0},{8,12},{12,8},{16,20},{20,16},{24,28},{28,24},{32,36},... | collective-permute-start | bytes 110600 | tf_op jit(solution)/shard_map/ppermute | solution.py:366
  67.5 18.3 %slice-start = ((f32[6,24,128]{2,1,0:T(8,128)}), f32[3,24,128]{2,1,0:T(8,128)S(1)}, s32[]{:S(2)}) async-start(f32[6,24,128]{2,1,0:T(8,128)} %copy-done), calls=%async_computation | async-start | bytes 73728 | tf_op jit(solution)/shard_map/slice | solution.py:404
  67.5 18.3 %collective-permute-start.7 = (f32[3,24,128]{2,1,0:T(8,128)S(1)}, f32[3,24,128]{2,1,0:T(8,128)S(1)}, u32[]{:S(2)}, u32[]{:S(2)}) collective-permute-start(f32[3,24,128]{2,1,0:T(8,128)S(1)} %get-tuple-element.21), channel_id=1, source_target_pairs={{4,8},{8,4},{12,16},{16,12},{20,24},{24,20},{28,32},{32,28},{36,40... | collective-permute-start | bytes 110600 | tf_op jit(solution)/shard_map/ppermute | solution.py:366
  85.7 0.8 slice-start.1

commit v3 on v2

--- a/solution.py
+++ b/solution.py
@@ -16,6 +16,7 @@
 RAW_A, RAW_W, RAW_Q, RAW_B = 0, 32, 48, 56
 RAW = 120
 BINS = 2 * ROWS
+SLOTS = 3
 BF = jnp.bfloat16
 F32 = jnp.float32
 
@@ -122,19 +123,16 @@
     return high, (scalar - high.astype(F32)).astype(BF)
 
 
-def pipelined(product, scalar, reduce, buffers):
-    for ref in buffers:
-        ref[...] = jnp.zeros_like(ref)
-
+def pipelined(product, scalar, reduce):
     def body(n, carry):
-        for half in (0, 1):
-            step = 2 * n + half
-            reduce(jnp.maximum(step - 2, 0), half)
-            product(jnp.minimum(step, DEPTH - 1), half)
-            scalar(jnp.clip(step - 1, 0, DEPTH - 1), 1 - half)
+        for part in range(SLOTS):
+            step = SLOTS * n + part
+            reduce(jnp.maximum(step - 2, 0), (part - 2) % SLOTS)
+            product(jnp.minimum(step, DEPTH - 1), part)
+            scalar(jnp.clip(step - 1, 0, DEPTH - 1), (part - 1) % SLOTS)
         return carry
 
-    lax.fori_loop(0, DEPTH // 2 + 1, body, 0)
+    lax.fori_loop(0, (DEPTH + 2) // SLOTS, body, 0)
 
 
 def inner_kernel(own, repulsion, acc, b_ref, raw, at_ref, w_ref, qi_ref, ut, sh):
@@ -221,7 +219,7 @@
         acc[row] = total[:, :128]
         acc[DEPTH + row] = total[:, 128:]
 
-    pipelined(product, scalar, reduce, (ut, sh))
+    pipelined(product, scalar, reduce)
 
 
 def outer_kernel(
@@ -284,7 +282,7 @@
                 w, sh[slot_id, side], preferred_element_type=F32
             )
 
-    pipelined(product, scalar, reduce, (ut, sh))
+    pipelined(product, scalar, reduce)
 
     flat = acc.reshape(2 * DEPTH * 16, 128)
     for group in range(4):
@@ -331,7 +329,7 @@
         in_specs=[VMEM, VMEM],
         out_specs=(VMEM, VMEM),
         scratch_shapes=FEATURES
-        + [pltpu.VMEM((2, 6, 128, 512), F32), pltpu.VMEM((2, 2, 768, 256), BF)],
+        + [pltpu.VMEM((SLOTS, 6, 128, 512), F32), pltpu.VMEM((SLOTS, 2, 768, 256), BF)],
         compiler_params=LIMIT,
         name=f"inner{step}",
     )(own, repulsion)
@@ -346,8 +344,8 @@
         out_specs=(VMEM, VMEM, VMEM),
         scratch_shapes=FEATURES
         + [
-            pltpu.VMEM((2, 6, 128, 256), F32),
-            pltpu.VMEM((2, 2, 768, 128), BF),
+            pltpu.VMEM((SLOTS, 6, 128, 256), F32),
+            pltpu.VMEM((SLOTS, 2, 768, 128), BF),
             pltpu.VMEM((2 * DEPTH, 16, 128), F32),
             pltpu.VMEM((BINS, 128), F32),
         ],
@@ -368,10 +366,19 @@
 
 def with_rows(block):
     count = lax.axis_size("gz")
-    up = [(i, i + 1) for i in range(count - 1)]
-    down = [(b, a) for a, b in up]
-    low = lax.ppermute(block[:, :, DEPTH - 1 :], "gz", up)
-    high = lax.ppermute(block[:, :, :1], "gz", down)
+    odd = lax.axis_index("gz") % 2 == 1
+    top, bottom = block[:, :, DEPTH - 1 :], block[:, :, :1]
+
+    def swapped(value, start):
+        route = []
+        for i in range(start, count - 1, 2):
+            route += [(i, i + 1), (i + 1, i)]
+        return lax.ppermute(value, "gz", route)
+
+    first = swapped(jnp.where(odd, bottom, top), 0)
+    second = swapped(jnp.where(odd, top, bottom), 1)
+    low = jnp.where(odd, first, second)
+    high = jnp.where(odd, second, first)
     pad = jnp.zeros(block.shape[:2] + (ROWS - USED, block.shape[3]), F32)
     return jnp.concatenate([block, low, high, pad], 2)
 

time: 95.2 us -> 91.2 us (0.958)
  the two profiles are of different devices: /device:TPU:1 before, /device:TPU:64 now
where the time goes in v3:
time: 91.2 us; the launch traced here: 90.6 us
  Pallas kernels  44.5 us (49%)
  starting transfers between devices  36.7 us (40%)
  waiting for transfers between devices  5.02 us (6%)
  local copies, waits for them, and re-layouts  2.29 us (3%)
  other arithmetic  1.15 us (1%)
  between operations  1.02 us (1%)
    pallas_call x2, Pallas kernels, inner_call(): pl.pallas_call(inner_kernel, out_shape=(jax.ShapeDtypeStruct((2 * DEPTH,...  29.7 us
    ppermute x4, starting transfers between devices, swap_pairs(): return lax.ppermute(value, 'gx', route)  18.4 us
    ppermute x4, starting transfers between devices, swapped(): return lax.ppermute(value, 'gz', route)  18.3 us
    pallas_call x2, Pallas kernels, outer_call(): pl.pallas_call(functools.partial(outer_kernel, step), out_shape=(out, out...  14.8 us
    ppermute x4, waiting for transfers between devices, swapped(): return lax.ppermute(value, 'gz', route)  5.01 us
  transfers between devices with their start and end apart: 8, of which 2 were waited for; matrix products, arithmetic and copies ran while one was open for 0% of the time, Pallas kernels for 33%

profile of v3, /device:TPU:64, one launch (start us, length us, event | category | flops | bytes accessed | tf_op | source)
XLA Modules:
  0.0 90.6 jit_solution(12599473017524602608)
XLA Ops:
  0.6 0.0 copy-start.7
  0.7 0.0 copy-start.9
  0.7 0.0 copy-start.8
  0.7 0.8 convert_element_type.12
  1.5 0.0 copy-start.6
  1.5 0.1 convert_element_type.13
  1.6 0.0 copy-done.7
  1.6 0.0 copy-done.9
  1.6 0.0 copy-start.4
  1.6 0.0 copy-start.5
  1.6 0.1 convert_bitcast_fusion
  1.7 0.0 copy-done.8
  1.7 0.1 pad_bitcast_fusion
  1.7 0.5 copy-done.6
  2.3 0.1 copy-done.4
  2.4 0.0 copy-done.5
  2.4 10.5 %collective-permute-start = (f32[6,2,1,128]{3,2,0,1:T(1,128)S(1)}, f32[6,2,1,128]{3,2,0,1:T(1,128)S(1)}, u32[]{:S(2)}, u32[]{:S(2)}) collective-permute-start(f32[6,2,1,128]{3,2,0,1:T(1,128)S(1)} %get-tuple-element.15), channel_id=1, source_target_pairs={{0,1},{1,0},{2,3},{3,2},{4,5},{5,4},{6,7},{7,6},{8,9},{9,8},{10,11... | collective-permute-start | bytes 18440 | tf_op jit(solution)/shard_map/ppermute | solution.py:376
  13.0 1.9 %collective-permute-start.1 = (f32[6,2,1,128]{3,2,0,1:T(1,128)S(1)}, f32[6,2,1,128]{3,2,0,1:T(1,128)S(1)}, u32[]{:S(2)}, u32[]{:S(2)}) collective-permute-start(f32[6,2,1,128]{3,2,0,1:T(1,128)S(1)} %broadcast_select_fusion.2), channel_id=1, source_target_pairs={{1,2},{2,1},{5,6},{6,5},{9,10},{10,9},{13,14},{14,13},{17,18},{18,... | collective-permute-start | bytes 18440 | tf_op jit(solution)/shard_map/ppermute | solution.py:376
  15.0 0.1 pad.24.clone
  15.0 0.0 collective-permute-done
  15.0 3.5 %collective-permute-done.1 = f32[6,2,1,128]{3,2,0,1:T(1,128)S(1)} collective-permute-done((f32[6,2,1,128]{3,2,0,1:T(1,128)S(1)}, f32[6,2,1,128]{3,2,0,1:T(1,128)S(1)}, u32[]{:S(2)}, u32[]{:S(2)}) %collective-permute-start.1) | collective-permute-done | bytes 6176 | tf_op jit(solution)/shard_map/ppermute | solution.py:376
  18.5 0.1 maximum_maximum_fusion
  18.6 0.0 copy-start.3
  18.7 1.9 %collective-permute-start.2 = (f32[6,24,128]{2,1,0:T(8,128)S(1)}, f32[6,24,128]{2,1,0:T(8,128)S(1)}, u32[]{:S(2)}, u32[]{:S(2)}) collective-permute-start(f32[6,24,128]{2,1,0:T(8,128)S(1)} %get-tuple-element.21), channel_id=1, source_target_pairs={{0,4},{4,0},{8,12},{12,8},{16,20},{20,16},{24,28},{28,24},{32,36},... | collective-permute-start | bytes 221192 | tf_op jit(solution)/shard_map/ppermute | solution.py:364
  20.6 11.2 %collective-permute-start.3 = (f32[6,24,128]{2,1,0:T(8,128)S(1)}, f32[6,24,128]{2,1,0:T(8,128)S(1)}, u32[]{:S(2)}, u32[]{:S(2)}) collective-permute-start(f32[6,24,128]{2,1,0:T(8,128)S(1)} %get-tuple-element.20), channel_id=1, source_target_pairs={{4,8},{8,4},{12,16},{16,12},{20,24},{24,20},{28,32},{32,28},{36,40... | collective-permute-start | bytes 221192 | tf_op jit(solution)/shard_map/ppermute | solution.py:364
  31.8 0.0 copy-start.2
  31.8 0.7 copy-done.2
  32.5 14.8 %inner0.1 = (f32[32,16,128]{2,1,0:T(8,128)S(1)}, bf16[48,80,128]{2,1,0:T(8,128)(2,1)S(1)}) custom-call(f32[6,2,24,128]{3,2,1,0:T(8,128)S(1)} %copy.16.own, f32[16,16]{1,0:T(8,128)S(1)} %copy-done.2), custom_call_target="tpu_custom_call" | custom-call | tf_op jit(solution)/shard_map/inner0/pallas_call | solution.py:323
  47.3 0.0 collective-permute-done.2.near
  47.3 0.0 copy-start
  47.3 0.0 collective-permute-done.3.far
  47.4 0.0 copy-start.1
  47.4 7.4 %outer0.1 = (f32[3,2,16,128]{3,2,1,0:T(8,128)S(1)}, f32[3,2,16,128]{3,2,1,0:T(8,128)S(1)}, f32[3,2,16,128]{3,2,1,0:T(8,128)}) custom-call(s32[1]{0:T(128)} %bitcast.parity, f32[6,2,24,128]{3,2,1,0:T(8,128)S(1)} %copy.16.own, f32[6,24,128]{2,1,0:T(8,128)S(1)} %collective-permute-done.2.near, f32[6,24,128]{2,1,0:T(8,128)S(1)} %collective-permute-done.3.far, ...), custom_call_target="tpu_custom_call" | custom-call | tf_op jit(solution)/shard_map/outer0/pallas_call | solution.py:340
  54.8 1.9 %collective-permute-start.4 = (f32[3,2,1,128]{3,2,0,1:T(1,128)S(1)}, f32[3,2,1,128]{3,2,0,1:T(1,128)S(1)}, u32[]{:S(2)}, u32[]{:S(2)}) collective-permute-start(f32[3,2,1,128]{3,2,0,1:T(1,128)S(1)} %get-tuple-element.24), channel_id=1, source_target_pairs={{0,1},{1,0},{2,3},{3,2},{4,5},{5,4},{6,7},{7,6},{8,9},{9,8},{10,11... | collective-permute-start | bytes 9224 | tf_op jit(solution)/shard_map/ppermute | solution.py:376
  56.7 3.9 %collective-permute-start.5 = (f32[3,2,1,128]{3,2,0,1:T(1,128)S(1)}, f32[3,2,1,128]{3,2,0,1:T(1,128)S(1)}, u32[]{:S(2)}, u32[]{:S(2)}) collective-permute-start(f32[3,2,1,128]{3,2,0,1:T(1,128)S(1)} %get-tuple-element.25), channel_id=1, source_target_pairs={{1,2},{2,1},{5,6},{6,5},{9,10},{10,9},{13,14},{14,13},{17,18},{18,... | collective-permute-start | bytes 9224 | tf_op jit(solution)/shard_map/ppermute | solution.py:376
  60.6 0.0 copy-done.3
  60.6 0.0 copy-done
  60.6 0.0 copy-done.1
  60.6 0.0 collective-permute-done.4
  60.7 1.5 %collective-permute-done.5 = f32[3,2,1,128]{3,2,0,1:T(1,128)S(1)} collective-permute-done((f32[3,2,1,128]{3,2,0,1:T(1,128)S(1)}, f32[3,2,1,128]{3,2,0,1:T(1,128)S(1)}, u32[]{:S(2)}, u32[]{:S(2)}) %collective-permute-start.5) | collective-permute-done | bytes 3104 | tf_op jit(solution)/shard_map/ppermute | solution.py:376
  62.2 0.0 slice-start.2
  62.2 1.9 %collective-permute-start.6 = (f32[3,24,128]{2,1,0:T(8,128)S(1)}, f32[3,24,128]{2,1,0:T(8,128)S(1)}, u32[]{:S(2)}, u32[]{:S(2)}) collective-permute-start(f32[3,24,128]{2,1,0:T(8,128)S(1)} %get-tuple-element.23), channel_id=1, source_target_pairs={{0,4},{4,0},{8,12},{12,8},{16,20},{20,16},{24,28},{28,24},{32,36},... | collective-permute-start | bytes 110600 | tf_op jit(solution)/shard_map/ppermute | solution.py:364
  64.2 0.0 slice-done.2
  64.2 0.0 slice-start
  64.2 3.4 %collective-permute-start.7 = (f32[3,24,128]{2,1,0:T(8,128)S(1)}, f32[3,24,128]{2,1,0:T(8,128)S(1)}, u32[]{:S(2)}, u32[]{:S(2)}) collective-permute-start(f32[3,24,128]{2,1,0:T(8,128)S(1)} %get-tuple-element.22), channel_id=1, source_target_pairs={{4,8},{8,4},{12,16},{16,12},{20,24},{24,20},{28,32},{32,28},{36,40... | collective-permute-start | bytes 110600 | tf_op jit(solution)/shard_map/ppermute | solution.py:364
  67.6 14.8 %inner1.1 = (f32[32,16,128]{2,1,0:T(8,128)S(1)}, bf16[48,80,128]{2,1,0:T(8,128)(2,1)S(1)}) custom-call(f32[6,2,24,128]{3,2,1,0:T(8,128)S(1)} %copy.22.own, f32[16,16]{1,0:T(8,128)S(1)} %copy-done.2), custom_call_target="tpu_custom_call" | custom-call | tf_op jit(solution)/shard_map/inner1/pallas_call | solution.py:323
  82.5 0.0 slice-start.1
  82.5 0.0 collective-permute-done.6
  82.5 0.0 slice-done
  82.5 0.0 collective-permute-done.7
  82.5 0.7 slice-done.1
  83.2 7.4 %outer1.1 = (f32[3,2,16,128]{3,2,1,0:T(8,128)}, f32[3,2,16,128]{3,2,1,0:T(8,128)}, f32[3,2,16,128]{3,2,1,0:T(8,128)}) custom-call(s32[1]{0:T(128)} %bitcast.parity, f32[6,2,24,128]{3,2,1,0:T(8,128)S(1)} %copy.22.own, f32[6,24,128]{2,1,0:T(8,128)S(1)} %pad_maximum_fusion.2.near, f32[6,24,128]{2,1,0:T(8,128)S(1)} %pad_maximum_fusion.3.far, ...), custom_call_target="tpu_custom_call" | custom-call | tf_op jit(solution)/shard_map/outer1/pallas_call | solution.py:340
  (17 shorter events, 0.2 us)
Async XLA Ops:
  0.6 0.9 %copy-start.7 = (s32[2,16,128]{2,1,0:T(8,128)S(1)}, s32[2,16,128]{2,1,0:T(8,128)}, u32[]{:S(2)}) copy-start(s32[2,16,128]{2,1,0:T(8,128)} %param.12) | copy-start | bytes 49156
  0.7 0.9 %copy-start.9 = (s32[2,16]{1,0:T(2,128)S(1)}, s32[2,16]{1,0:T(2,128)}, u32[]{:S(2)}) copy-start(s32[2,16]{1,0:T(2,128)} %param.13) | copy-start | bytes 388
  0.7 1.0 %copy-start.8 = (f32[2,16,128]{2,1,0:T(8,128)S(1)}, f32[2,16,128]{2,1,0:T(8,128)}, u32[]{:S(2)}) copy-start(f32[2,16,128]{2,1,0:T(8,128)} %param.11) | copy-start | bytes 49156
  1.5 0.8 copy-start.6
  1.6 0.8 copy-start.4
  1.6 0.8 copy-start.5
  2.4 12.6 %collective-permute-start = (f32[6,2,1,128]{3,2,0,1:T(1,128)S(1)}, f32[6,2,1,128]{3,2,0,1:T(1,128)S(1)}, u32[]{:S(2)}, u32[]{:S(2)}) collective-permute-start(f32[6,2,1,128]{3,2,0,1:T(1,128)S(1)} %get-tuple-element.15), channel_id=1, source_target_pairs={{0,1},{1,0},{2,3},{3,2},{4,5},{5,4},{6,7},{7,6},{8,9},{9,8},{10,11... | collective-permute-start | bytes 18440 | tf_op jit(solution)/shard_map/ppermute | solution.py:376
  13.0 5.5 %collective-permute-start.1 = (f32[6,2,1,128]{3,2,0,1:T(1,128)S(1)}, f32[6,2,1,128]{3,2,0,1:T(1,128)S(1)}, u32[]{:S(2)}, u32[]{:S(2)}) collective-permute-start(f32[6,2,1,128]{3,2,0,1:T(1,128)S(1)} %broadcast_select_fusion.2), channel_id=1, source_target_pairs={{1,2},{2,1},{5,6},{6,5},{9,10},{10,9},{13,14},{14,13},{17,18},{18,... | collective-permute-start | bytes 18440 | tf_op jit(solution)/shard_map/ppermute | solution.py:376
  18.6 42.0 %copy-start.3 = (f32[6,2,24,128]{3,2,0,1:T(8,128)}, f32[6,2,24,128]{3,2,0,1:T(8,128)S(1)}, u32[]{:S(2)}) copy-start(f32[6,2,24,128]{3,2,0,1:T(8,128)S(1)} %maximum_maximum_fusion) | copy-start | bytes 442372
  18.7 28.7 %collective-permute-start.2 = (f32[6,24,128]{2,1,0:T(8,128)S(1)}, f32[6,24,128]{2,1,0:T(8,128)S(1)}, u32[]{:S(2)}, u32[]{:S(2)}) collective-permute-start(f32[6,24,128]{2,1,0:T(8,128)S(1)} %get-tuple-element.21), channel_id=1, source_target_pairs={{0,4},{4,0},{8,12},{12,8},{16,20},{20,16},{24,28},{28,24},{32,36},... | collective-permute-start | bytes 221192 | tf_op jit(solution)/shard_map/ppermute | solution.py:364
  20.6 26.8 %collective-permute-start.3 = (f32[6,24,128]{2,1,0:T(8,128)S(1)}, f32[6,24,128]{2,1,0:T(8,128)S(1)}, u32[]{:S(2)}, u32[]{:S(2)}) collective-permute-start(f32[6,24,128]{2,1,0:T(8,128)S(1)} %get-tuple-element.20), channel_id=1, source_target_pairs={{4,8},{8,4},{12,16},{16,12},{20,24},{24,20},{28,32},{32,28},{36,40... | collective-permute-start | bytes 221192 | tf_op jit(solution)/shard_map/ppermute | solution.py:364
  31.8 0.7 copy-start.2
  47.3 13.3 %copy-start = (f32[6,24,128]{2,1,0:T(8,128)}, f32[6,24,128]{2,1,0:T(8,128)S(1)}, u32[]{:S(2)}) copy-start(f32[6,24,128]{2,1,0:T(8,128)S(1)} %collective-permute-done.2.near) | copy-start | bytes 221188
  47.4 13.3 %copy-start.1 = (f32[6,24,128]{2,1,0:T(8,128)}, f32[6,24,128]{2,1,0:T(8,128)S(1)}, u32[]{:S(2)}) copy-start(f32[6,24,128]{2,1,0:T(8,128)S(1)} %collective-permute-done.3.far) | copy-start | bytes 221188
  54.8 5.9 %collective-permute-start.4 = (f32[3,2,1,128]{3,2,0,1:T(1,128)S(1)}, f32[3,2,1,128]{3,2,0,1:T(1,128)S(1)}, u32[]{:S(2)}, u32[]{:S(2)}) collective-permute-start(f32[3,2,1,128]{3,2,0,1:T(1,128)S(1)} %get-tuple-element.24), channel_id=1, source_target_pairs={{0,1},{1,0},{2,3},{3,2},{4,5},{5,4},{6,7},{7,6},{8,9},{9,8},{10,11... | collective-permute-start | bytes 9224 | tf_op jit(solution)/shard_map/ppermute | solution.py:376
  56.7 5.5 %collective-permute-start.5 = (f32[3,2,1,128]{3,2,0,1:T(1,128)S(1)}, f32[3,2,1,128]{3,2,0,1:T(1,128)S(1)}, u32[]{:S(2)}, u32[]{:S(2)}) collective-permute-start(f32[3,2,1,128]{3,2,0,1:T(1,128)S(1)} %get-tuple-element.25), channel_id=1, source_target_pairs={{1,2},{2,1},{5,6},{6,5},{9,10},{10,9},{13,14},{14,13},{17,18},{18,... | collective-permute-start | bytes 9224 | tf_op jit(solution)/shard_map/ppermute | solution.py:376
  62.2 2.0 %slice-start.2 = ((f32[6,2,24,128]{3,2,0,1:T(8,128)}), f32[3,2,24,128]{3,2,0,1:T(8,128)S(1)}, s32[]{:S(2)}) async-start(f32[6,2,24,128]{3,2,0,1:T(8,128)} %copy-done.3), calls=%async_computation.2 | async-start | bytes 147456 | tf_op jit(solution)/shard_map/slice | solution.py:410
  62.2 20.2 %collective-permute-start.6 = (f32[3,24,128]{2,1,0:T(8,128)S(1)}, f32[3,24,128]{2,1,0:T(8,128)S(1)}, u32[]{:S(2)}, u32[]{:S(2)}) collective-permute-start(f32[3,24,128]{2,1,0:T(8,128)S(1)} %get-tuple-element.23), channel_id=1, source_target_pairs={{0,4},{4,0},{8,12},{12,8},{16,20},{20,16},{24,28},{28,24},{32,36},... | collective-permute-start | bytes 110600 | tf_op jit(solution)/shard_map/ppermute | solution.py:364
  64.2 18.3 %slice-start = ((f32[6,24,128]{2,1,0:T(8,128)}), f32[3,24,128]{2,1,0:T(8,128)S(1)}, s32[]{:S(2)}) async-start(f32[6,24,128]{2,1,0:T(8,128)} %copy-done), calls=%async_computation | async-start | bytes 73728 | tf_op jit(solution)/shard_map/slice | solution.py:411
  64.2 18.3 %collective-permute-start.7 = (f32[3,24,128]{2,1,0:T(8,128)S(1)}, f32[3,24,128]{2,1,0:T(8,128)S(1)}, u32[]{:S(2)}, u32[]{:S(2)}) collective-permute-start(f32[3,24,128]{2,1,0:T(8,128)S(1)} %get-tuple-element.22), channel_id=1, source_target_pairs={{4,8},{8,4},{12,16},{16,12},{20,24},{24,20},{28,32},{32,28},{36,40... | collective-permute-start | bytes 110600 | tf_op jit(solution)/shard_map/ppermute | solution.py:364
  82.5 0.8 slice-start.1
